TPU v7x, 32 devices: a whole 2x2x4 slice. The times are simulated.
32 devices in a mesh: seq: 32 (over z, y, x, core).
Axes of the slice: x: 2, y: 2, z: 4, core: 2. Of those that a mesh axis runs over, the one named last changes fastest.
Arguments:
- tokens: bfloat16 [4096, 1024], P('seq'), may hold values from -96 to 96
- query_weight: bfloat16 [1024, 1024], replicated, may hold values from -1 to 1
- key_weight: bfloat16 [1024, 512], replicated, may hold values from -1 to 1
- value_matrix: bfloat16 [1024, 512], replicated, may hold values from -0.1875 to 0.1875
- out_weight: bfloat16 [1024, 1024], replicated, may hold values from -0.1875 to 0.1875
- out_cotangent: bfloat16 [4096, 1024], P('seq'), may hold values from -6 to 6
Outputs:
- attn_out: bfloat16 [4096, 1024], P('seq')
- tokens_grad: bfloat16 [4096, 1024], P('seq')
- query_weight_grad: float32 [1024, 1024], P('seq')
- key_weight_grad: float32 [1024, 512], P('seq')
- value_weight_grad: float32 [1024, 512], P('seq')
- out_weight_grad: float32 [1024, 1024], P(None, 'seq')
All inputs are finite; a program needn't handle non-finite values.
Results may differ from a plain program's by a relative error of at most 0.015.
The roundings to bfloat16 on the way count: a program that leaves them out, or rounds other values in their place, can miss the bound.
Values may be sent and summed in bfloat16 or wider, within the bound.
A program may use at most 128 MiB of HBM per device.

v0:
```python
import jax
import jax.numpy as jnp
from jax import lax
from jax.sharding import PartitionSpec as P

QUERY_HEADS = 16
KEY_HEADS = 8
HEAD_SIZE = 64
QUERY_PER_KEY = 2


SCALE = 0.125
MASKED = -1e30
CONTRACT_ROWS = (((0,), (0,)), ((), ()))


def passed_along(block, axis, distance):
    devices = range(lax.axis_size(axis))
    route = [(i - distance, i) for i in devices if i - distance in devices]
    return lax.ppermute(block, axis, route)


def split_queries(weight_matrix):
    return jnp.transpose(
        weight_matrix.reshape(weight_matrix.shape[0], KEY_HEADS, QUERY_PER_KEY, HEAD_SIZE),
        (1, 0, 2, 3),
    )


def split_keys(weight_matrix):
    return jnp.transpose(
        weight_matrix.reshape(weight_matrix.shape[0], KEY_HEADS, HEAD_SIZE), (1, 0, 2)
    )


def join_queries(head_rows):
    return jnp.transpose(head_rows, (1, 0, 2, 3)).reshape(
        head_rows.shape[1], QUERY_HEADS * HEAD_SIZE
    )


def join_keys(head_rows):
    return jnp.transpose(head_rows, (1, 0, 2)).reshape(head_rows.shape[1], KEY_HEADS * HEAD_SIZE)


def head_scores(queries, key_head, allowed):
    scores = (
        jnp.einsum("tgd,wd->tgw", queries, key_head, preferred_element_type=jnp.float32) * SCALE
    )
    return jnp.where(allowed[:, None, :], scores, MASKED)


def head_forward(queries, key_head, value_head, allowed):
    scores = head_scores(queries, key_head, allowed)
    highest = jnp.max(scores, axis=-1, keepdims=True)
    summed_total = jnp.sum(jnp.exp(scores - highest), axis=-1, keepdims=True)
    logsum = highest + jnp.log(summed_total)
    probs = jnp.exp(scores - logsum).astype(jnp.bfloat16)
    attended = jnp.einsum(
        "tgw,wd->tgd", probs, value_head, preferred_element_type=jnp.float32
    ).astype(jnp.bfloat16)
    return (attended, logsum[..., 0])


def head_backward(queries, key_head, value_head, logsum, d_attended, attended, allowed):
    scores = head_scores(queries, key_head, allowed)
    weights = jnp.exp(scores - logsum[..., None])
    probs = weights.astype(jnp.bfloat16)
    spread = jnp.sum(d_attended.astype(jnp.float32) * attended.astype(jnp.float32), axis=-1)
    value_part = jnp.einsum("tgw,tgd->wd", probs, d_attended, preferred_element_type=jnp.float32)
    dprobs = jnp.einsum("tgd,wd->tgw", d_attended, value_head, preferred_element_type=jnp.float32)
    dscores = (weights * (dprobs - spread[..., None])).astype(jnp.bfloat16)
    query_piece = (
        jnp.einsum("tgw,wd->tgd", dscores, key_head, preferred_element_type=jnp.float32) * SCALE
    )
    key_piece = (
        jnp.einsum("tgw,tgd->wd", dscores, queries, preferred_element_type=jnp.float32) * SCALE
    )
    return (query_piece, key_piece, value_part)


def transposed_rows(left_side, right_side):
    return lax.dot_general(left_side, right_side, CONTRACT_ROWS, preferred_element_type=jnp.float32)


def shards(tokens, query_weight, key_weight, value_matrix, out_weight, out_cotangent):
    local_rows = tokens.shape[0]
    queries = jnp.dot(tokens, query_weight, preferred_element_type=jnp.float32).astype(jnp.bfloat16)
    keys_own = jnp.dot(tokens, key_weight, preferred_element_type=jnp.float32).astype(jnp.bfloat16)
    values_own = jnp.dot(tokens, value_matrix, preferred_element_type=jnp.float32).astype(
        jnp.bfloat16
    )
    near_keys, near_values = passed_along((keys_own, values_own), "seq", 1)
    far_keys, far_values = passed_along((keys_own, values_own), "seq", 2)
    key_window = jnp.concatenate([far_keys, near_keys, keys_own], axis=0)
    value_window = jnp.concatenate([far_values, near_values, values_own], axis=0)
    shard_idx = lax.axis_index("seq")
    query_pos = shard_idx * local_rows + lax.iota(jnp.int32, local_rows)
    key_pos = (shard_idx - 2) * local_rows + lax.iota(jnp.int32, 3 * local_rows)
    allowed = (key_pos[None, :] <= query_pos[:, None]) & (key_pos[None, :] >= 0)
    q_heads = split_queries(queries)
    k_heads = split_keys(key_window)
    v_heads = split_keys(value_window)
    att_heads, logsum = lax.map(
        lambda operands: head_forward(operands[0], operands[1], operands[2], allowed),
        (q_heads, k_heads, v_heads),
    )
    attended = join_queries(att_heads)
    attn_out = jnp.dot(attended, out_weight, preferred_element_type=jnp.float32).astype(
        jnp.bfloat16
    )
    d_attended = jnp.dot(out_cotangent, out_weight.T, preferred_element_type=jnp.float32).astype(
        jnp.bfloat16
    )
    q_part, k_part, v_part = lax.map(
        lambda operands: head_backward(
            operands[0], operands[1], operands[2], operands[3], operands[4], operands[5], allowed
        ),
        (q_heads, k_heads, v_heads, logsum, split_queries(d_attended), att_heads),
    )
    query_grad = join_queries(q_part).astype(jnp.bfloat16)
    key_parts = join_keys(k_part)
    value_parts = join_keys(v_part)
    far_key_part = key_parts[:local_rows]
    near_key_part = key_parts[local_rows : 2 * local_rows]
    own_key_part = key_parts[2 * local_rows :]
    far_value_part = value_parts[:local_rows]
    near_value_part = value_parts[local_rows : 2 * local_rows]
    own_value_part = value_parts[2 * local_rows :]
    near_back_keys, near_back_values = passed_along((near_key_part, near_value_part), "seq", -1)
    far_back_keys, far_back_values = passed_along((far_key_part, far_value_part), "seq", -2)
    key_grad = (own_key_part + near_back_keys + far_back_keys).astype(jnp.bfloat16)
    value_grad = (own_value_part + near_back_values + far_back_values).astype(jnp.bfloat16)
    tokens_grad = (
        jnp.dot(query_grad, query_weight.T, preferred_element_type=jnp.float32)
        + jnp.dot(key_grad, key_weight.T, preferred_element_type=jnp.float32)
        + jnp.dot(value_grad, value_matrix.T, preferred_element_type=jnp.float32)
    ).astype(jnp.bfloat16)
    query_weight_grad = lax.psum_scatter(
        transposed_rows(tokens, query_grad), "seq", scatter_dimension=0, tiled=True
    )
    key_weight_grad = lax.psum_scatter(
        transposed_rows(tokens, key_grad), "seq", scatter_dimension=0, tiled=True
    )
    value_weight_grad = lax.psum_scatter(
        transposed_rows(tokens, value_grad), "seq", scatter_dimension=0, tiled=True
    )
    out_rows_local = lax.psum_scatter(
        transposed_rows(out_cotangent, attended), "seq", scatter_dimension=0, tiled=True
    )
    out_weight_grad = out_rows_local.T
    return (
        attn_out,
        tokens_grad,
        query_weight_grad,
        key_weight_grad,
        value_weight_grad,
        out_weight_grad,
    )


def solution(mesh):
    in_specs = (P("seq", None), P(), P(), P(), P(), P("seq", None))
    out_specs = (
        P("seq", None),
        P("seq", None),
        P("seq", None),
        P("seq", None),
        P("seq", None),
        P(None, "seq"),
    )
    return jax.shard_map(shards, mesh=mesh, in_specs=in_specs, out_specs=out_specs, check_vma=False)
```

profile of v0, /device:TPU:0, one launch (start us, length us, event | category | flops | bytes accessed | tf_op | source)
XLA Modules:
  0.0 691.9 jit_solution(16490356631593237039)
XLA Ops:
  7.2 1.8 convolution_convert_fusion.5
  9.1 5.0 collective-permute-start
  14.1 2.1 collective-permute-start.1
  16.2 1.6 convolution_convert_fusion.4
  17.8 3.9 collective-permute-start.2
  21.7 3.9 collective-permute-start.3
  25.6 2.0 convolution_convert_fusion.3
  31.5 1.8 pad_maximum_fusion.1
  33.3 1.2 copy.30
  34.5 23.2 %while.28 = (s32[]{:T(128)}, bf16[8,128,2,64]{1,3,2,0:T(8,128)(2,1)}, f32[8,128,2]{1,2,0:T(2,128)}, bf16[8,128,2,64]{1,3,2,0:T(8,128)(2,1)}, bf16[8,384,64]{1,2,...) while((s32[]{:T(128)}, ...), condition=%wide.region_3.4_spmd.clone, body=%wide.region_0.3_spmd.clone.sunk | while | flops 25968384 | bytes 1455077 | solution.py:104
  34.6 1.1 fusion.105
  37.5 1.1 fusion.105
  40.4 1.1 fusion.105
  46.2 1.1 fusion.105
  49.1 1.1 fusion.105
  52.0 1.1 fusion.105
  54.9 1.1 fusion.105
  57.7 48.5 %while.29 = (s32[]{:T(128)}, bf16[8,128,2,64]{1,3,2,0:T(8,128)(2,1)}, f32[8,384,64]{1,2,0:T(8,128)}, f32[8,384,64]{1,2,0:T(8,128)}, bf16[8,128,2,64]{1,3,2,0:T(8...) while((s32[]{:T(128)}, ...), condition=%wide.region_6.7_spmd.clone, body=%wide.region_4.6_spmd.clone.sunk | while | flops 63807232 | bytes 2486797 | solution.py:115
  60.6 1.6 fusion.122
  66.6 1.6 fusion.122
  72.7 1.6 fusion.122
  78.7 1.6 fusion.122
  84.8 1.6 fusion.122
  90.9 1.6 fusion.122
  96.9 1.6 fusion.122
  103.0 1.6 fusion.122
  106.2 1.2 fusion.55
  107.4 1.3 collective-permute-start.6
  108.7 1.3 collective-permute-start.7
  110.8 9.4 %collective-permute-done.7 = f32[128,512]{0,1:T(8,128)S(1)} collective-permute-done((f32[128,512]{0,1:T(8,128)S(1)}, f32[128,512]{0,1:T(8,128)S(1)}, u32[]{:S(2)}, u32[]{:S(2)}) %collective-permute-start.7) | collective-permute-done | bytes 262176 | tf_op jit(solution)/shard_map/ppermute | solution.py:20
  120.3 1.8 convolution_bitcast_fusion.4
  122.0 2.9 copy.40
  126.2 1.3 collective-permute-start.4
  127.5 1.3 collective-permute-start.5
  129.6 11.7 %collective-permute-done.5 = f32[128,512]{0,1:T(8,128)S(1)} collective-permute-done((f32[128,512]{0,1:T(8,128)S(1)}, f32[128,512]{0,1:T(8,128)S(1)}, u32[]{:S(2)}, u32[]{:S(2)}) %collective-permute-start.5) | collective-permute-done | bytes 262176 | tf_op jit(solution)/shard_map/ppermute | solution.py:20
  141.3 1.8 convolution_bitcast_fusion.5
  143.1 2.9 copy.38
  146.1 3.6 convolution_bitcast_fusion.3
  149.7 5.4 copy.36
  156.1 2.7 convolution_bitcast_fusion.2
  158.8 5.4 copy.42
  164.2 1.2 convolution_convert_fusion.2
  165.9 1.9 fusion.57
  168.4 1.2 fusion.49
  169.6 95.8 %reduce-scatter.17.cloned.1.call-done = f32[32,512]{1,0:T(8,128)} async-done(((f32[1024,512]{1,0:T(8,128)}), f32[32,512]{1,0:T(8,128)}) %reduce-scatter.17.cloned.1.call-update) | async-done | bytes 65552
  265.4 137.1 %reduce-scatter.15.cloned.1.call-done = f32[32,512]{1,0:T(8,128)} async-done(((f32[1024,512]{1,0:T(8,128)}), f32[32,512]{1,0:T(8,128)}) %reduce-scatter.15.cloned.1.call-update) | async-done | bytes 65552
  402.5 141.6 %reduce-scatter.13.cloned.1.call-done = f32[32,1024]{1,0:T(8,128)} async-done(((f32[1024,1024]{1,0:T(8,128)}), f32[32,1024]{1,0:T(8,128)}) %reduce-scatter.13.cloned.1.call-update) | async-done | bytes 131088
  544.1 141.3 %reduce-scatter.19.cloned.1.call-done = f32[32,1024]{1,0:T(8,128)} async-done(((f32[1024,1024]{1,0:T(8,128)}), f32[32,1024]{1,0:T(8,128)}) %reduce-scatter.19.cloned.1.call-update) | async-done | bytes 131088
  (142 shorter events, 60.0 us)
Async XLA Ops:
  7.2 20.4 %copy-start = (bf16[1024,1024]{1,0:T(8,128)(2,1)S(1)}, bf16[1024,1024]{1,0:T(8,128)(2,1)}, u32[]{:S(2)}) copy-start(bf16[1024,1024]{1,0:T(8,128)(2,1)} %param.14) | copy-start | bytes 6291460
  7.2 18.4 %copy-start.1 = (bf16[128,1024]{1,0:T(8,128)(2,1)S(1)}, bf16[128,1024]{1,0:T(8,128)(2,1)}, u32[]{:S(2)}) copy-start(bf16[128,1024]{1,0:T(8,128)(2,1)} %param.10) | copy-start | bytes 786436
  7.2 258.2 %reduce-scatter.17.cloned.1.call-start = ((), (), s32[]{:S(2)}) async-start(), calls=%async_computation.6 | async-start | bytes 2162688
  9.0 19.4 %copy-start.9 = (bf16[128,512]{1,0:T(8,128)(2,1)}, bf16[128,512]{1,0:T(8,128)(2,1)S(1)}, u32[]{:S(2)}) copy-start(bf16[128,512]{1,0:T(8,128)(2,1)S(1)} %convolution_convert_fusion.5) | copy-start | bytes 393220
  9.0 18.6 %copy-start.6 = (bf16[128,1024]{1,0:T(8,128)(2,1)S(1)}, bf16[128,1024]{1,0:T(8,128)(2,1)}, u32[]{:S(2)}) copy-start(bf16[128,1024]{1,0:T(8,128)(2,1)} %param.15) | copy-start | bytes 786436
  9.1 20.5 %collective-permute-start = (bf16[128,512]{1,0:T(8,128)(2,1)S(1)}, bf16[128,512]{1,0:T(8,128)(2,1)S(1)}, u32[]{:S(2)}, u32[]{:S(2)}) collective-permute-start(bf16[128,512]{1,0:T(8,128)(2,1)S(1)} %convolution_convert_fusion.5), channel_id=1, source_target_pairs={{0,2},{1,3},{2,4},{3,5},{4,6},{5,7},{6,8},{7,9},{8,10},{9,11},{10,... | collective-permute-start | bytes 393224 | tf_op jit(solution)/shard_map/ppermute | solution.py:20
  14.1 16.2 %collective-permute-start.1 = (bf16[128,512]{1,0:T(8,128)(2,1)S(1)}, bf16[128,512]{1,0:T(8,128)(2,1)}, u32[]{:S(2)}, u32[]{:S(2)}) collective-permute-start(bf16[128,512]{1,0:T(8,128)(2,1)S(1)} %convolution_convert_fusion.5), channel_id=1, source_target_pairs={{0,1},{1,2},{2,3},{3,4},{4,5},{5,6},{6,7},{7,8},{8,9},{9,10},{10,1... | collective-permute-start | bytes 393224 | tf_op jit(solution)/shard_map/ppermute | solution.py:20
  17.8 13.7 %collective-permute-start.2 = (bf16[128,512]{1,0:T(8,128)(2,1)S(1)}, bf16[128,512]{1,0:T(8,128)(2,1)}, u32[]{:S(2)}, u32[]{:S(2)}) collective-permute-start(bf16[128,512]{1,0:T(8,128)(2,1)S(1)} %convolution_convert_fusion.4), channel_id=1, source_target_pairs={{0,2},{1,3},{2,4},{3,5},{4,6},{5,7},{6,8},{7,9},{8,10},{9,11},{10,... | collective-permute-start | bytes 393224 | tf_op jit(solution)/shard_map/ppermute | solution.py:20
  21.7 9.8 %collective-permute-start.3 = (bf16[128,512]{1,0:T(8,128)(2,1)S(1)}, bf16[128,512]{1,0:T(8,128)(2,1)}, u32[]{:S(2)}, u32[]{:S(2)}) collective-permute-start(bf16[128,512]{1,0:T(8,128)(2,1)S(1)} %convolution_convert_fusion.4), channel_id=1, source_target_pairs={{0,1},{1,2},{2,3},{3,4},{4,5},{5,6},{6,7},{7,8},{8,9},{9,10},{10,1... | collective-permute-start | bytes 393224 | tf_op jit(solution)/shard_map/ppermute | solution.py:20
  29.6 0.7 copy-start.10
  107.4 3.4 collective-permute-start.6
  108.7 11.6 %collective-permute-start.7 = (f32[128,512]{0,1:T(8,128)S(1)}, f32[128,512]{0,1:T(8,128)S(1)}, u32[]{:S(2)}, u32[]{:S(2)}) collective-permute-start(f32[128,512]{0,1:T(8,128)S(1)} %bitcast.194), channel_id=1, source_target_pairs={{2,0},{3,1},{4,2},{5,3},{6,4},{7,5},{8,6},{9,7},{10,8},{11,9},{12,... | collective-permute-start | bytes 786440 | tf_op jit(solution)/shard_map/ppermute | solution.py:20
  124.9 1.1 copy-start.8
  125.0 277.5 %reduce-scatter.15.cloned.1.call-start = ((), (), s32[]{:S(2)}) async-start(), calls=%async_computation.5 | async-start | bytes 2162688
  126.2 3.4 collective-permute-start.4
  127.5 13.8 %collective-permute-start.5 = (f32[128,512]{0,1:T(8,128)S(1)}, f32[128,512]{0,1:T(8,128)S(1)}, u32[]{:S(2)}, u32[]{:S(2)}) collective-permute-start(f32[128,512]{0,1:T(8,128)S(1)} %bitcast.195), channel_id=1, source_target_pairs={{2,0},{3,1},{4,2},{5,3},{6,4},{7,5},{8,6},{9,7},{10,8},{11,9},{12,... | collective-permute-start | bytes 786440 | tf_op jit(solution)/shard_map/ppermute | solution.py:20
  146.0 398.1 %reduce-scatter.13.cloned.1.call-start = ((), (), s32[]{:S(2)}) async-start(), calls=%async_computation.4 | async-start | bytes 4325376
  155.1 0.9 copy-start.5
  155.1 1.0 copy-start.7
  155.1 530.3 %reduce-scatter.19.cloned.1.call-start = ((), (), s32[]{:S(2)}) async-start(), calls=%async_computation.7 | async-start | bytes 4325376
  164.2 1.7 copy-start.2
  165.9 2.0 copy-start.3
  165.9 2.5 copy-start.4
Sparse Core Ops, SparseCore 0:
  125.1 140.2 reduce-scatter.16
  268.2 134.2 reduce-scatter.14
  405.4 138.7 reduce-scatter.12
  546.8 138.5 reduce-scatter.18
where the time goes:
time: 695 us; the launch traced here: 692 us
  waiting for transfers between devices  539 us (78%)
  matrix products  72.5 us (10%)
  local copies, waits for them, and re-layouts  28.9 us (4%)
  starting transfers between devices  20.2 us (3%)
  other arithmetic  17.2 us (2%)
  between operations  14.1 us (2%)
    unnamed x8, waiting for transfers between devices  516 us
    ppermute x8, waiting for transfers between devices, passed_along(): return lax.ppermute(block, axis, route)  22.8 us
    ppermute x8, starting transfers between devices, passed_along(): return lax.ppermute(block, axis, route)  20 us
    unnamed x26, local copies, waits for them, and re-layouts  19.8 us
    dot_general x16, matrix products, head_scores(): jnp.einsum('tgd,wd->tgw', queries, key_head, preferred_element_type=jnp.f...  17 us
  transfers between devices with their start and end apart: 12, of which 8 were waited for; matrix products, arithmetic and copies ran while one was open for 5% of the time, Pallas kernels for 0%

commit v1 on v0

v1 whole, which is shorter than its diff:
```python
import jax
import jax.numpy as jnp
from jax import lax
from jax.experimental import pallas as pl
from jax.experimental.pallas import tpu as pltpu
from jax.sharding import PartitionSpec as P

HEAD_SIZE = 64
SCALE = 0.125
MASKED = -1e30
BF16 = jnp.bfloat16
F32 = jnp.float32


def dot(left, right, dims):
    return lax.dot_general(left, right, (dims, ((), ())), preferred_element_type=F32)


NN = ((1,), (0,))
NT = ((1,), (1,))
TN = ((0,), (0,))


def passed_along(block, axis, distance):
    devices = range(lax.axis_size(axis))
    route = [(i - distance, i) for i in devices if i - distance in devices]
    return lax.ppermute(block, axis, route)


def attention_kernel(
    q_ref, own_ref, near_ref, far_ref, d_ref, att_ref, qg_ref, own_out, near_out, far_out
):
    rows = q_ref.shape[0]
    key_columns = own_ref.shape[1] // 2
    window = 3 * rows
    shard = lax.axis_index("seq")
    query_row = lax.broadcasted_iota(jnp.int32, (2 * rows, window), 0)
    query_row = jnp.where(query_row >= rows, query_row - rows, query_row)
    key_row = lax.broadcasted_iota(jnp.int32, (2 * rows, window), 1)
    allowed = (key_row <= query_row + 2 * rows) & (key_row >= (2 - shard) * rows)

    def both_heads(ref, g):
        tile = ref[:, g * 2 * HEAD_SIZE : (g + 1) * 2 * HEAD_SIZE]
        return jnp.concatenate([tile[:, :HEAD_SIZE], tile[:, HEAD_SIZE:]], axis=0)

    def side_by_side(stacked):
        return jnp.concatenate([stacked[:rows], stacked[rows:]], axis=1)

    def one_group(g, keys, values):
        queries = both_heads(q_ref, g)
        d_att = both_heads(d_ref, g)
        scores = jnp.where(allowed, dot(queries, keys, NT) * SCALE, MASKED)
        highest = jnp.max(scores, axis=-1, keepdims=True)
        raised = jnp.exp(scores - highest)
        weights = raised * (1.0 / jnp.sum(raised, axis=-1, keepdims=True))
        probs = weights.astype(BF16)
        attended = dot(probs, values, NN).astype(BF16)
        spread = jnp.sum(d_att.astype(F32) * attended.astype(F32), axis=-1, keepdims=True)
        dprobs = dot(d_att, values, NT)
        dscores = (weights * (dprobs - spread)).astype(BF16)
        q_grad = (dot(dscores, keys, NN) * SCALE).astype(BF16)
        tile = slice(g * 2 * HEAD_SIZE, (g + 1) * 2 * HEAD_SIZE)
        att_ref[:, tile] = side_by_side(attended)
        qg_ref[:, tile] = side_by_side(q_grad)
        return dot(dscores, queries, TN) * SCALE, dot(probs, d_att, TN)

    for pair in range(key_columns // (2 * HEAD_SIZE)):
        tile = slice(pair * 2 * HEAD_SIZE, (pair + 1) * 2 * HEAD_SIZE)
        value_tile = slice(key_columns + tile.start, key_columns + tile.stop)
        sides = (far_ref, near_ref, own_ref)
        keys = jnp.concatenate([ref[:, tile] for ref in sides], axis=0)
        values = jnp.concatenate([ref[:, value_tile] for ref in sides], axis=0)
        k_low, v_low = one_group(2 * pair, keys[:, :HEAD_SIZE], values[:, :HEAD_SIZE])
        k_high, v_high = one_group(2 * pair + 1, keys[:, HEAD_SIZE:], values[:, HEAD_SIZE:])
        for where, low, high in ((tile, k_low, k_high), (value_tile, v_low, v_high)):
            part = jnp.concatenate([low, high], axis=1)
            far_out[:, where] = part[:rows].astype(BF16)
            near_out[:, where] = part[rows : 2 * rows].astype(BF16)
            own_out[:, where] = part[2 * rows :]


def attention(queries, own, near, far, d_attended):
    shape = jax.ShapeDtypeStruct
    vmem = pl.BlockSpec(memory_space=pltpu.VMEM)
    return pl.pallas_call(
        attention_kernel,
        out_shape=(
            shape(queries.shape, BF16),
            shape(queries.shape, BF16),
            shape(own.shape, F32),
            shape(own.shape, BF16),
            shape(own.shape, BF16),
        ),
        in_specs=[vmem] * 5,
        out_specs=(vmem,) * 5,
        cost_estimate=pl.CostEstimate(
            flops=10**9, bytes_accessed=4 * 10**6, transcendentals=10**6
        ),
        name="attention",
    )(queries, own, near, far, d_attended)


def scattered_sum(partial, axis, order):
    n = lax.axis_size(axis)
    me = lax.axis_index(axis)
    left = list(reversed(range(n.bit_length() - 1)))
    held = partial.reshape((2,) * len(left) + (partial.shape[0] // n, partial.shape[1]))
    for bit in order:
        at = left.index(bit)
        left.pop(at)
        mine = (me >> bit) & 1
        sent = lax.dynamic_index_in_dim(held, 1 - mine, at, keepdims=False).astype(BF16)
        kept = lax.dynamic_index_in_dim(held, mine, at, keepdims=False)
        got = lax.ppermute(sent, axis, [(i, i ^ (1 << bit)) for i in range(n)])
        held = kept.astype(F32) + got.astype(F32)
    return held


def shards(tokens, query_weight, key_weight, value_matrix, out_weight, out_cotangent):
    keys = dot(tokens, key_weight, NN).astype(BF16)
    values = dot(tokens, value_matrix, NN).astype(BF16)
    own = jnp.concatenate([keys, values], axis=1)
    near = passed_along(own, "seq", 1)
    far = passed_along(own, "seq", 2)
    queries = dot(tokens, query_weight, NN).astype(BF16)
    d_attended = dot(out_cotangent, out_weight, NT).astype(BF16)
    attended, query_grad, own_part, near_part, far_part = attention(
        queries, own, near, far, d_attended
    )
    near_back = passed_along(near_part, "seq", -1)
    far_back = passed_along(far_part, "seq", -2)
    bits = lax.axis_size("seq").bit_length() - 1
    rest = list(range(1, bits))
    orders = ([0] + rest, [0] + rest[1:] + rest[:1], [0] + rest[2:] + rest[:2])
    out_rows = scattered_sum(dot(out_cotangent, attended, TN), "seq", orders[0])
    query_rows = scattered_sum(dot(tokens, query_grad, TN), "seq", orders[1])
    attn_out = dot(attended, out_weight, NN).astype(BF16)
    both_grad = (own_part + near_back.astype(F32) + far_back.astype(F32)).astype(BF16)
    both_rows = scattered_sum(dot(tokens, both_grad, TN), "seq", orders[2])
    width = key_weight.shape[1]
    tokens_grad = (
        dot(query_grad, query_weight, NT)
        + dot(both_grad[:, :width], key_weight, NT)
        + dot(both_grad[:, width:], value_matrix, NT)
    ).astype(BF16)
    return (
        attn_out,
        tokens_grad,
        query_rows,
        both_rows[:, :width],
        both_rows[:, width:],
        out_rows.T,
    )


def solution(mesh):
    in_specs = (P("seq", None), P(), P(), P(), P(), P("seq", None))
    out_specs = (
        P("seq", None),
        P("seq", None),
        P("seq", None),
        P("seq", None),
        P("seq", None),
        P(None, "seq"),
    )
    return jax.shard_map(shards, mesh=mesh, in_specs=in_specs, out_specs=out_specs, check_vma=False)
```

time: 695 us -> 104 us (0.15)
  waiting for transfers between devices: 539 us -> 42.5 us
  matrix products: 72.5 us -> 14.6 us
  local copies, waits for them, and re-layouts: 28.9 us -> 2.42 us
  other arithmetic: 17.2 us -> 3.51 us
  between operations: 14.1 us -> 1.1 us
  starting transfers between devices: 20.2 us -> 30.8 us
  Pallas kernels: 0 us -> 8.95 us
    unnamed x8 -> x0, waiting for transfers between devices: 516 us -> none
    dot_general x68 -> x11, matrix products: 72.5 us -> 14.6 us  [dot(): lax.dot_general(left, right, (dims, ((), ())), preferred_element_type=F32)]
    ppermute x0 -> x15, waiting for transfers between devices: none -> 37.7 us  [scattered_sum(): got = lax.ppermute(sent, axis, [(i, i ^ 1 << bit) for i in range(n)])]
    ppermute x0 -> x15, starting transfers between devices: none -> 21.2 us  [scattered_sum(): got = lax.ppermute(sent, axis, [(i, i ^ 1 << bit) for i in range(n)])]
    unnamed x26 -> x24, local copies, waits for them, and re-layouts: 19.8 us -> 0.79 us
    ppermute x8 -> x4, waiting for transfers between devices: 22.8 us -> 4.79 us  [passed_along(): return lax.ppermute(block, axis, route)]
    ppermute x8 -> x4, starting transfers between devices: 20 us -> 9.56 us  [passed_along(): return lax.ppermute(block, axis, route)]
    pallas_call x0 -> x1, Pallas kernels: none -> 8.95 us  [attention(): pl.pallas_call(attention_kernel, out_shape=(shape(queries.shape, BF16), s...]
  transfers between devices with their start and end apart: 12 -> 19, of which waited for: 8 -> 8; matrix products, arithmetic and copies ran while one was open for 5% -> 15% of each run, Pallas kernels for 0% -> 0%
where the time goes in v1:
time: 104 us
  waiting for transfers between devices  42.5 us (41%)
  starting transfers between devices  30.8 us (30%)
  matrix products  14.6 us (14%)
  Pallas kernels  8.95 us (9%)
  other arithmetic  3.51 us (3%)
  local copies, waits for them, and re-layouts  2.42 us (2%)
  between operations  1.1 us (1%)
    ppermute x15, waiting for transfers between devices, scattered_sum(): got = lax.ppermute(sent, axis, [(i, i ^ 1 << bit) for i in range(n)])  37.7 us
    ppermute x15, starting transfers between devices, scattered_sum(): got = lax.ppermute(sent, axis, [(i, i ^ 1 << bit) for i in range(n)])  21.2 us
    dot_general x11, matrix products, dot(): lax.dot_general(left, right, (dims, ((), ())), preferred_element_type=F32)  14.6 us
    ppermute x4, starting transfers between devices, passed_along(): return lax.ppermute(block, axis, route)  9.56 us
    pallas_call x1, Pallas kernels, attention(): pl.pallas_call(attention_kernel, out_shape=(shape(queries.shape, BF16), s...  8.95 us
    ppermute x4, waiting for transfers between devices, passed_along(): return lax.ppermute(block, axis, route)  4.79 us
    add x14, other arithmetic, scattered_sum(): held = kept.astype(F32) + got.astype(F32)  2.73 us
  transfers between devices with their start and end apart: 19, of which 8 were waited for; matrix products, arithmetic and copies ran while one was open for 15% of the time, Pallas kernels for 0%

profile of v1, /device:TPU:0, one launch (start us, length us, event | category | flops | bytes accessed | tf_op | source)
XLA Modules:
  0.0 103.8 jit_solution(17361502411458726902)
XLA Ops:
  0.7 1.8 %convolution_convert_fusion.3 = bf16[128,512]{1,0:T(8,128)(2,1)S(1)} fusion(bf16[128,1024]{1,0:T(8,128)(2,1)} %param.6, bf16[1024,512]{1,0:T(8,128)(2,1)} %param.9), kind=kOutput, calls=%fused_computation.12 | convolution fusion | flops 134283264 | bytes 1441792 | tf_op jit(solution)/shard_map/dot_general | solution.py:16
  2.4 1.7 %convolution_convert_fusion.4 = bf16[128,512]{1,0:T(8,128)(2,1)S(1)} fusion(bf16[128,1024]{1,0:T(8,128)(2,1)} %param.6, bf16[1024,512]{1,0:T(8,128)(2,1)} %param.8), kind=kOutput, calls=%fused_computation.13 | convolution fusion | flops 134283264 | bytes 1441792 | tf_op jit(solution)/shard_map/dot_general | solution.py:16
  4.1 2.4 %collective-permute-start = (bf16[128,1024]{1,0:T(8,128)(2,1)S(1)}, bf16[128,1024]{1,0:T(8,128)(2,1)S(1)}, u32[]{:S(2)}, u32[]{:S(2)}) collective-permute-start(bf16[128,1024]{1,0:T(8,128)(2,1)S(1)} %pad_maximum_fusion.own_ref), channel_id=1, source_target_pairs={{0,1},{1,2},{2,3},{3,4},{4,5},{5,6},{6,7},{7,8},{8,9},{9,10},{10,1... | collective-permute-start | bytes 786440 | tf_op jit(solution)/shard_map/ppermute | solution.py:27
  6.6 4.4 %collective-permute-start.1 = (bf16[128,1024]{1,0:T(8,128)(2,1)S(1)}, bf16[128,1024]{1,0:T(8,128)(2,1)S(1)}, u32[]{:S(2)}, u32[]{:S(2)}) collective-permute-start(bf16[128,1024]{1,0:T(8,128)(2,1)S(1)} %pad_maximum_fusion.own_ref), channel_id=1, source_target_pairs={{0,2},{1,3},{2,4},{3,5},{4,6},{5,7},{6,8},{7,9},{8,10},{9,11},{10,... | collective-permute-start | bytes 786440 | tf_op jit(solution)/shard_map/ppermute | solution.py:27
  11.0 2.7 %convolution_convert_fusion.2.q_ref = bf16[128,1024]{1,0:T(8,128)(2,1)} fusion(bf16[128,1024]{1,0:T(8,128)(2,1)S(1)} %copy-done.2, bf16[1024,1024]{1,0:T(8,128)(2,1)} %param.7), kind=kOutput, calls=%fused_computation.11 | convolution fusion | flops 268566528 | bytes 2621440 | tf_op jit(solution)/shard_map/dot_general | solution.py:16
  13.8 1.5 %convolution_convert_fusion.1.d_ref = bf16[128,1024]{1,0:T(8,128)(2,1)} fusion(bf16[128,1024]{1,0:T(8,128)(2,1)S(1)} %copy-done.6, bf16[1024,1024]{1,0:T(8,128)(2,1)S(1)} %copy-done), kind=kOutput, calls=%fused_computation.10 | convolution fusion | flops 268566528 | bytes 2621440 | tf_op jit(solution)/shard_map/dot_general | solution.py:16
  15.3 2.3 %collective-permute-done.1.far_ref = bf16[128,1024]{1,0:T(8,128)(2,1)S(1)} collective-permute-done((bf16[128,1024]{1,0:T(8,128)(2,1)S(1)}, bf16[128,1024]{1,0:T(8,128)(2,1)S(1)}, u32[]{:S(2)}, u32[]{:S(2)}) %collective-permute-start.1) | collective-permute-done | bytes 262176 | tf_op jit(solution)/shard_map/ppermute | solution.py:27
  17.6 0.7 copy-done.11
  18.4 8.9 %attention.1 = (bf16[128,1024]{1,0:T(8,128)(2,1)}, bf16[128,1024]{1,0:T(8,128)(2,1)}, f32[128,1024]{1,0:T(8,128)}, bf16[128,1024]{1,0:T(8,128)(2,1)}, bf16[128,1024]{1,0:T(8,128)(2,1)}) custom-call(bf16[128,1024]{1,0:T(8,128)(2,1)} %convolution_convert_fusion.2.q_ref, bf16[128,1024]{1,0:T(8,128)(2,1)} %copy-done.9, bf16[128,1024]{1,0:T(8,128)(2,1)} %copy-done.10, ...), custom_call_target="tpu_custom_call" | custom-call | flops 1000000000 | bytes 4000000 | tf_op jit(solution)/shard_map/attention/pallas_call | solution.py:85
  27.3 1.3 %collective-permute-start.3 = (bf16[128,1024]{1,0:T(8,128)(2,1)}, bf16[128,1024]{1,0:T(8,128)(2,1)S(1)}, u32[]{:S(2)}, u32[]{:S(2)}) collective-permute-start(bf16[128,1024]{1,0:T(8,128)(2,1)} %get-tuple-element.15), channel_id=1, source_target_pairs={{2,0},{3,1},{4,2},{5,3},{6,4},{7,5},{8,6},{9,7},{10,8},{11,9},{12,... | collective-permute-start | bytes 786440 | tf_op jit(solution)/shard_map/ppermute | solution.py:27
  28.6 1.5 %collective-permute-start.2 = (bf16[128,1024]{1,0:T(8,128)(2,1)}, bf16[128,1024]{1,0:T(8,128)(2,1)S(1)}, u32[]{:S(2)}, u32[]{:S(2)}) collective-permute-start(bf16[128,1024]{1,0:T(8,128)(2,1)} %get-tuple-element.14), channel_id=1, source_target_pairs={{1,0},{2,1},{3,2},{4,3},{5,4},{6,5},{7,6},{8,7},{9,8},{10,9},{11,1... | collective-permute-start | bytes 786440 | tf_op jit(solution)/shard_map/ppermute | solution.py:27
  30.1 1.7 %fusion.23 = f32[1024,1024]{0,1:T(8,128)S(1)} fusion(bf16[128,1024]{1,0:T(8,128)(2,1)} %get-tuple-element.12, bf16[128,1024]{1,0:T(8,128)(2,1)S(1)} %copy-done.2), kind=kOutput, calls=%fused_computation.67 | convolution fusion | flops 268435456 | bytes 4718592 | tf_op jit(solution)/shard_map/dot_general | solution.py:16
  31.8 0.2 fusion.2
  32.0 1.2 %collective-permute-start.4 = (bf16[2,2,2,2,32,1024]{5,4,3,0,1,2:T(8,128)(2,1)S(1)}, bf16[2,2,2,2,32,1024]{5,4,3,0,1,2:T(8,128)(2,1)S(1)}, u32[]{:S(2)}, u32[]{:S(2)}) collective-permute-start(bf16[2,2,2,2,32,1024]{5,4,3,0,1,2:T(8,128)(2,1)S(1)} %fusion.2), channel_id=1, source_target_pairs={{0,1},{1,0},{2,3},{3,2},{4,5},{5,4},{6,7},{7,6},{8,9},{9,8},{10,11... | collective-permute-start | bytes 3145736 | tf_op jit(solution)/shard_map/ppermute | solution.py:114
  33.2 0.8 fusion.25
  33.9 0.2 fusion.4
  34.1 0.8 collective-permute-start.14
  34.9 1.2 %convolution_convert_fusion = bf16[128,1024]{1,0:T(8,128)(2,1)} fusion(bf16[128,1024]{1,0:T(8,128)(2,1)S(1)} %copy-done.7, bf16[1024,1024]{1,0:T(8,128)(2,1)S(1)} %copy-done), kind=kOutput, calls=%fused_computation.9 | convolution fusion | flops 268566528 | bytes 2621440 | tf_op jit(solution)/shard_map/dot_general | solution.py:16
  36.0 2.5 %collective-permute-done.3 = bf16[128,1024]{1,0:T(8,128)(2,1)S(1)} collective-permute-done((bf16[128,1024]{1,0:T(8,128)(2,1)}, bf16[128,1024]{1,0:T(8,128)(2,1)S(1)}, u32[]{:S(2)}, u32[]{:S(2)}) %collective-permute-start.3) | collective-permute-done | bytes 262176 | tf_op jit(solution)/shard_map/ppermute | solution.py:27
  38.6 0.5 fusion.14
  39.1 0.8 fusion.24
  39.9 0.2 fusion.3
  40.1 2.7 %collective-permute-start.9 = (bf16[2,2,2,2,32,1024]{5,4,2,3,0,1:T(8,128)(2,1)S(1)}, bf16[2,2,2,2,32,1024]{5,4,2,3,0,1:T(8,128)(2,1)S(1)}, u32[]{:S(2)}, u32[]{:S(2)}) collective-permute-start(bf16[2,2,2,2,32,1024]{5,4,2,3,0,1:T(8,128)(2,1)S(1)} %fusion.3), channel_id=1, source_target_pairs={{0,1},{1,0},{2,3},{3,2},{4,5},{5,4},{6,7},{7,6},{8,9},{9,8},{10,11... | collective-permute-start | bytes 3145736 | tf_op jit(solution)/shard_map/ppermute | solution.py:114
  42.8 0.5 fusion.16
  43.2 1.6 %fusion.1 = bf16[128,1024]{1,0:T(8,128)(2,1)} fusion(f32[128,1024]{1,0:T(8,128)S(1)} %fusion.14, f32[128,1024]{1,0:T(8,128)S(1)} %fusion.16, bf16[128,1024]{1,0:T(8,128)(2,1)S(1)} %copy-done.5, bf16[1024,1024]{1,0:T(8,128)(2,1)S(1)} %copy-done.1), kind=kOutput, calls=%fused_computation.8 | convolution fusion | flops 268828672 | bytes 3670016 | tf_op jit(solution)/shard_map/dot_general | solution.py:16
  44.8 0.5 bitcast_add_fusion.2
  45.4 2.7 %collective-permute-start.5 = (bf16[2,2,2,32,1024]{4,3,2,0,1:T(8,128)(2,1)S(1)}, bf16[2,2,2,32,1024]{4,3,2,0,1:T(8,128)(2,1)S(1)}, u32[]{:S(2)}, u32[]{:S(2)}) collective-permute-start(bf16[2,2,2,32,1024]{4,3,2,0,1:T(8,128)(2,1)S(1)} %fusion.5), channel_id=1, source_target_pairs={{0,4},{1,5},{2,6},{3,7},{4,0},{5,1},{6,2},{7,3},{8,12},{9,13},{10,... | collective-permute-start | bytes 1572872 | tf_op jit(solution)/shard_map/ppermute | solution.py:114
  48.1 0.5 bitcast_add_fusion
  48.6 2.4 %collective-permute-start.15 = (bf16[2,2,2,32,1024]{4,3,0,1,2:T(8,128)(2,1)S(1)}, bf16[2,2,2,32,1024]{4,3,0,1,2:T(8,128)(2,1)S(1)}, u32[]{:S(2)}, u32[]{:S(2)}) collective-permute-start(bf16[2,2,2,32,1024]{4,3,0,1,2:T(8,128)(2,1)S(1)} %fusion.7), channel_id=1, source_target_pairs={{0,2},{1,3},{2,0},{3,1},{4,6},{5,7},{6,4},{7,5},{8,10},{9,11},{10,... | collective-permute-start | bytes 1572872 | tf_op jit(solution)/shard_map/ppermute | solution.py:114
  51.1 0.5 bitcast_add_fusion.1
  51.6 1.7 %collective-permute-start.10 = (bf16[2,2,2,32,1024]{4,3,1,2,0:T(8,128)(2,1)S(1)}, bf16[2,2,2,32,1024]{4,3,1,2,0:T(8,128)(2,1)S(1)}, u32[]{:S(2)}, u32[]{:S(2)}) collective-permute-start(bf16[2,2,2,32,1024]{4,3,1,2,0:T(8,128)(2,1)S(1)} %fusion.6), channel_id=1, source_target_pairs={{0,8},{1,9},{2,10},{3,11},{4,12},{5,13},{6,14},{7,15},{8,0},{9,1},... | collective-permute-start | bytes 1572872 | tf_op jit(solution)/shard_map/ppermute | solution.py:114
  53.3 7.4 %collective-permute-done.5 = bf16[2,2,2,32,1024]{4,3,2,0,1:T(8,128)(2,1)S(1)} collective-permute-done((bf16[2,2,2,32,1024]{4,3,2,0,1:T(8,128)(2,1)S(1)}, bf16[2,2,2,32,1024]{4,3,2,0,1:T(8,128)(2,1)S(1)}, u32[]{:S(2)}, u32[]{:S(2)}) %collective-permute-start.5) | collective-permute-done | bytes 524320 | tf_op jit(solution)/shard_map/ppermute | solution.py:114
  60.8 3.2 %collective-permute-start.6 = (bf16[2,2,32,1024]{3,2,1,0:T(8,128)(2,1)S(1)}, bf16[2,2,32,1024]{3,2,1,0:T(8,128)(2,1)S(1)}, u32[]{:S(2)}, u32[]{:S(2)}) collective-permute-start(bf16[2,2,32,1024]{3,2,1,0:T(8,128)(2,1)S(1)} %fusion.8), channel_id=1, source_target_pairs={{0,8},{1,9},{2,10},{3,11},{4,12},{5,13},{6,14},{7,15},{8,0},{9,1},... | collective-permute-start | bytes 786440 | tf_op jit(solution)/shard_map/ppermute | solution.py:114
  64.2 0.7 collective-permute-start.16
  64.9 6.6 %collective-permute-done.6 = bf16[2,2,32,1024]{3,2,1,0:T(8,128)(2,1)S(1)} collective-permute-done((bf16[2,2,32,1024]{3,2,1,0:T(8,128)(2,1)S(1)}, bf16[2,2,32,1024]{3,2,1,0:T(8,128)(2,1)S(1)}, u32[]{:S(2)}, u32[]{:S(2)}) %collective-permute-start.6) | collective-permute-done | bytes 262176 | tf_op jit(solution)/shard_map/ppermute | solution.py:114
  71.6 2.7 %collective-permute-start.7 = (bf16[2,32,1024]{2,1,0:T(8,128)(2,1)S(1)}, bf16[2,32,1024]{2,1,0:T(8,128)(2,1)S(1)}, u32[]{:S(2)}, u32[]{:S(2)}) collective-permute-start(bf16[2,32,1024]{2,1,0:T(8,128)(2,1)S(1)} %fusion.11), channel_id=1, source_target_pairs={{0,16},{1,17},{2,18},{3,19},{4,20},{5,21},{6,22},{7,23},{8,24},{9,... | collective-permute-start | bytes 393224 | tf_op jit(solution)/shard_map/ppermute | solution.py:114
  74.4 0.4 collective-permute-start.11
  74.9 1.7 %collective-permute-start.17 = (bf16[2,32,1024]{2,1,0:T(8,128)(2,1)S(1)}, bf16[2,32,1024]{2,1,0:T(8,128)(2,1)S(1)}, u32[]{:S(2)}, u32[]{:S(2)}) collective-permute-start(bf16[2,32,1024]{2,1,0:T(8,128)(2,1)S(1)} %fusion.13), channel_id=1, source_target_pairs={{0,8},{1,9},{2,10},{3,11},{4,12},{5,13},{6,14},{7,15},{8,0},{9,1},... | collective-permute-start | bytes 393224 | tf_op jit(solution)/shard_map/ppermute | solution.py:114
  76.6 10.4 %collective-permute-done.7 = bf16[2,32,1024]{2,1,0:T(8,128)(2,1)S(1)} collective-permute-done((bf16[2,32,1024]{2,1,0:T(8,128)(2,1)S(1)}, bf16[2,32,1024]{2,1,0:T(8,128)(2,1)S(1)}, u32[]{:S(2)}, u32[]{:S(2)}) %collective-permute-start.7) | collective-permute-done | bytes 131104 | tf_op jit(solution)/shard_map/ppermute | solution.py:114
  87.0 0.4 collective-permute-start.8
  87.5 0.2 collective-permute-start.18
  87.6 5.9 %collective-permute-done.11 = bf16[2,2,32,1024]{3,2,0,1:T(8,128)(2,1)S(1)} collective-permute-done((bf16[2,2,32,1024]{3,2,0,1:T(8,128)(2,1)S(1)}, bf16[2,2,32,1024]{3,2,0,1:T(8,128)(2,1)S(1)}, u32[]{:S(2)}, u32[]{:S(2)}) %collective-permute-start.11) | collective-permute-done | bytes 262176 | tf_op jit(solution)/shard_map/ppermute | solution.py:114
  93.8 0.7 bitcast_add_fusion.14
  94.5 4.3 %collective-permute-done.12 = bf16[2,32,1024]{2,1,0:T(8,128)(2,1)S(1)} collective-permute-done((bf16[2,32,1024]{2,1,0:T(8,128)(2,1)S(1)}, bf16[2,32,1024]{2,1,0:T(8,128)(2,1)S(1)}, u32[]{:S(2)}, u32[]{:S(2)}) %collective-permute-start.12) | collective-permute-done | bytes 131104 | tf_op jit(solution)/shard_map/ppermute | solution.py:114
  98.8 0.5 collective-permute-start.13
  99.3 0.7 fusion.18
  100.0 3.1 %collective-permute-done.13 = bf16[32,1024]{1,0:T(8,128)(2,1)S(1)} collective-permute-done((bf16[32,1024]{1,0:T(8,128)(2,1)S(1)}, bf16[32,1024]{1,0:T(8,128)(2,1)S(1)}, u32[]{:S(2)}, u32[]{:S(2)}) %collective-permute-start.13) | collective-permute-done | bytes 65568 | tf_op jit(solution)/shard_map/ppermute | solution.py:114
  103.1 0.7 fusion.22
  (59 shorter events, 1.4 us)
Async XLA Ops:
  0.6 13.1 %copy-start = (bf16[1024,1024]{1,0:T(8,128)(2,1)S(1)}, bf16[1024,1024]{1,0:T(8,128)(2,1)}, u32[]{:S(2)}) copy-start(bf16[1024,1024]{1,0:T(8,128)(2,1)} %param.10) | copy-start | bytes 6291460
  0.6 10.3 %copy-start.2 = (bf16[128,1024]{1,0:T(8,128)(2,1)S(1)}, bf16[128,1024]{1,0:T(8,128)(2,1)}, u32[]{:S(2)}) copy-start(bf16[128,1024]{1,0:T(8,128)(2,1)} %param.6) | copy-start | bytes 786436
  2.4 11.3 %copy-start.6 = (bf16[128,1024]{1,0:T(8,128)(2,1)S(1)}, bf16[128,1024]{1,0:T(8,128)(2,1)}, u32[]{:S(2)}) copy-start(bf16[128,1024]{1,0:T(8,128)(2,1)} %param.11) | copy-start | bytes 786436
  4.1 11.2 %copy-start.9 = (bf16[128,1024]{1,0:T(8,128)(2,1)}, bf16[128,1024]{1,0:T(8,128)(2,1)S(1)}, u32[]{:S(2)}) copy-start(bf16[128,1024]{1,0:T(8,128)(2,1)S(1)} %pad_maximum_fusion.own_ref) | copy-start | bytes 786436
  4.1 11.1 %collective-permute-start = (bf16[128,1024]{1,0:T(8,128)(2,1)S(1)}, bf16[128,1024]{1,0:T(8,128)(2,1)S(1)}, u32[]{:S(2)}, u32[]{:S(2)}) collective-permute-start(bf16[128,1024]{1,0:T(8,128)(2,1)S(1)} %pad_maximum_fusion.own_ref), channel_id=1, source_target_pairs={{0,1},{1,2},{2,3},{3,4},{4,5},{5,6},{6,7},{7,8},{8,9},{9,10},{10,1... | collective-permute-start | bytes 786440 | tf_op jit(solution)/shard_map/ppermute | solution.py:27
  6.6 11.1 %collective-permute-start.1 = (bf16[128,1024]{1,0:T(8,128)(2,1)S(1)}, bf16[128,1024]{1,0:T(8,128)(2,1)S(1)}, u32[]{:S(2)}, u32[]{:S(2)}) collective-permute-start(bf16[128,1024]{1,0:T(8,128)(2,1)S(1)} %pad_maximum_fusion.own_ref), channel_id=1, source_target_pairs={{0,2},{1,3},{2,4},{3,5},{4,6},{5,7},{6,8},{7,9},{8,10},{9,11},{10,... | collective-permute-start | bytes 786440 | tf_op jit(solution)/shard_map/ppermute | solution.py:27
  15.3 2.3 %copy-start.10 = (bf16[128,1024]{1,0:T(8,128)(2,1)}, bf16[128,1024]{1,0:T(8,128)(2,1)S(1)}, u32[]{:S(2)}) copy-start(bf16[128,1024]{1,0:T(8,128)(2,1)S(1)} %collective-permute-done.near_ref) | copy-start | bytes 786436
  17.6 0.7 copy-start.11
  27.3 11.2 %collective-permute-start.3 = (bf16[128,1024]{1,0:T(8,128)(2,1)}, bf16[128,1024]{1,0:T(8,128)(2,1)S(1)}, u32[]{:S(2)}, u32[]{:S(2)}) collective-permute-start(bf16[128,1024]{1,0:T(8,128)(2,1)} %get-tuple-element.15), channel_id=1, source_target_pairs={{2,0},{3,1},{4,2},{5,3},{6,4},{7,5},{8,6},{9,7},{10,8},{11,9},{12,... | collective-permute-start | bytes 786440 | tf_op jit(solution)/shard_map/ppermute | solution.py:27
  28.6 9.9 %collective-permute-start.2 = (bf16[128,1024]{1,0:T(8,128)(2,1)}, bf16[128,1024]{1,0:T(8,128)(2,1)S(1)}, u32[]{:S(2)}, u32[]{:S(2)}) collective-permute-start(bf16[128,1024]{1,0:T(8,128)(2,1)} %get-tuple-element.14), channel_id=1, source_target_pairs={{1,0},{2,1},{3,2},{4,3},{5,4},{6,5},{7,6},{8,7},{9,8},{10,9},{11,1... | collective-permute-start | bytes 786440 | tf_op jit(solution)/shard_map/ppermute | solution.py:27
  31.8 1.4 %copy-start.7 = (bf16[128,1024]{1,0:T(8,128)(2,1)S(1)}, bf16[128,1024]{1,0:T(8,128)(2,1)}, u32[]{:S(2)}) copy-start(bf16[128,1024]{1,0:T(8,128)(2,1)} %get-tuple-element.11) | copy-start | bytes 786436
  32.0 12.9 %collective-permute-start.4 = (bf16[2,2,2,2,32,1024]{5,4,3,0,1,2:T(8,128)(2,1)S(1)}, bf16[2,2,2,2,32,1024]{5,4,3,0,1,2:T(8,128)(2,1)S(1)}, u32[]{:S(2)}, u32[]{:S(2)}) collective-permute-start(bf16[2,2,2,2,32,1024]{5,4,3,0,1,2:T(8,128)(2,1)S(1)} %fusion.2), channel_id=1, source_target_pairs={{0,1},{1,0},{2,3},{3,2},{4,5},{5,4},{6,7},{7,6},{8,9},{9,8},{10,11... | collective-permute-start | bytes 3145736 | tf_op jit(solution)/shard_map/ppermute | solution.py:114
  33.9 4.6 %copy-start.8 = (f32[128,1024]{1,0:T(8,128)S(1)}, f32[128,1024]{1,0:T(8,128)}, u32[]{:S(2)}) copy-start(f32[128,1024]{1,0:T(8,128)} %get-tuple-element.13) | copy-start | bytes 1572868
  34.1 4.5 %copy-start.3 = (bf16[1024,512]{1,0:T(8,128)(2,1)S(1)}, bf16[1024,512]{1,0:T(8,128)(2,1)}, u32[]{:S(2)}) copy-start(bf16[1024,512]{1,0:T(8,128)(2,1)} %param.9) | copy-start | bytes 3145732
  34.1 14.0 %collective-permute-start.14 = (bf16[2,2,2,2,32,1024]{5,4,0,1,2,3:T(8,128)(2,1)S(1)}, bf16[2,2,2,2,32,1024]{5,4,0,1,2,3:T(8,128)(2,1)S(1)}, u32[]{:S(2)}, u32[]{:S(2)}) collective-permute-start(bf16[2,2,2,2,32,1024]{5,4,0,1,2,3:T(8,128)(2,1)S(1)} %fusion.4), channel_id=1, source_target_pairs={{0,1},{1,0},{2,3},{3,2},{4,5},{5,4},{6,7},{7,6},{8,9},{9,8},{10,11... | collective-permute-start | bytes 3145736 | tf_op jit(solution)/shard_map/ppermute | solution.py:114
  39.1 3.7 %copy-start.4 = (bf16[1024,512]{1,0:T(8,128)(2,1)S(1)}, bf16[1024,512]{1,0:T(8,128)(2,1)}, u32[]{:S(2)}) copy-start(bf16[1024,512]{1,0:T(8,128)(2,1)} %param.8) | copy-start | bytes 3145732
  39.9 3.4 %copy-start.1 = (bf16[1024,1024]{1,0:T(8,128)(2,1)S(1)}, bf16[1024,1024]{1,0:T(8,128)(2,1)}, u32[]{:S(2)}) copy-start(bf16[1024,1024]{1,0:T(8,128)(2,1)} %param.7) | copy-start | bytes 6291460
  39.9 3.4 %copy-start.5 = (bf16[128,1024]{1,0:T(8,128)(2,1)S(1)}, bf16[128,1024]{1,0:T(8,128)(2,1)}, u32[]{:S(2)}) copy-start(bf16[128,1024]{1,0:T(8,128)(2,1)} %get-tuple-element.12) | copy-start | bytes 786436
  40.1 11.0 %collective-permute-start.9 = (bf16[2,2,2,2,32,1024]{5,4,2,3,0,1:T(8,128)(2,1)S(1)}, bf16[2,2,2,2,32,1024]{5,4,2,3,0,1:T(8,128)(2,1)S(1)}, u32[]{:S(2)}, u32[]{:S(2)}) collective-permute-start(bf16[2,2,2,2,32,1024]{5,4,2,3,0,1:T(8,128)(2,1)S(1)} %fusion.3), channel_id=1, source_target_pairs={{0,1},{1,0},{2,3},{3,2},{4,5},{5,4},{6,7},{7,6},{8,9},{9,8},{10,11... | collective-permute-start | bytes 3145736 | tf_op jit(solution)/shard_map/ppermute | solution.py:114
  45.4 15.3 %collective-permute-start.5 = (bf16[2,2,2,32,1024]{4,3,2,0,1:T(8,128)(2,1)S(1)}, bf16[2,2,2,32,1024]{4,3,2,0,1:T(8,128)(2,1)S(1)}, u32[]{:S(2)}, u32[]{:S(2)}) collective-permute-start(bf16[2,2,2,32,1024]{4,3,2,0,1:T(8,128)(2,1)S(1)} %fusion.5), channel_id=1, source_target_pairs={{0,4},{1,5},{2,6},{3,7},{4,0},{5,1},{6,2},{7,3},{8,12},{9,13},{10,... | collective-permute-start | bytes 1572872 | tf_op jit(solution)/shard_map/ppermute | solution.py:114
  48.6 15.4 %collective-permute-start.15 = (bf16[2,2,2,32,1024]{4,3,0,1,2:T(8,128)(2,1)S(1)}, bf16[2,2,2,32,1024]{4,3,0,1,2:T(8,128)(2,1)S(1)}, u32[]{:S(2)}, u32[]{:S(2)}) collective-permute-start(bf16[2,2,2,32,1024]{4,3,0,1,2:T(8,128)(2,1)S(1)} %fusion.7), channel_id=1, source_target_pairs={{0,2},{1,3},{2,0},{3,1},{4,6},{5,7},{6,4},{7,5},{8,10},{9,11},{10,... | collective-permute-start | bytes 1572872 | tf_op jit(solution)/shard_map/ppermute | solution.py:114
  51.6 22.6 %collective-permute-start.10 = (bf16[2,2,2,32,1024]{4,3,1,2,0:T(8,128)(2,1)S(1)}, bf16[2,2,2,32,1024]{4,3,1,2,0:T(8,128)(2,1)S(1)}, u32[]{:S(2)}, u32[]{:S(2)}) collective-permute-start(bf16[2,2,2,32,1024]{4,3,1,2,0:T(8,128)(2,1)S(1)} %fusion.6), channel_id=1, source_target_pairs={{0,8},{1,9},{2,10},{3,11},{4,12},{5,13},{6,14},{7,15},{8,0},{9,1},... | collective-permute-start | bytes 1572872 | tf_op jit(solution)/shard_map/ppermute | solution.py:114
  60.8 10.6 %collective-permute-start.6 = (bf16[2,2,32,1024]{3,2,1,0:T(8,128)(2,1)S(1)}, bf16[2,2,32,1024]{3,2,1,0:T(8,128)(2,1)S(1)}, u32[]{:S(2)}, u32[]{:S(2)}) collective-permute-start(bf16[2,2,32,1024]{3,2,1,0:T(8,128)(2,1)S(1)} %fusion.8), channel_id=1, source_target_pairs={{0,8},{1,9},{2,10},{3,11},{4,12},{5,13},{6,14},{7,15},{8,0},{9,1},... | collective-permute-start | bytes 786440 | tf_op jit(solution)/shard_map/ppermute | solution.py:114
  64.2 10.6 %collective-permute-start.16 = (bf16[2,2,32,1024]{3,2,0,1:T(8,128)(2,1)S(1)}, bf16[2,2,32,1024]{3,2,0,1:T(8,128)(2,1)S(1)}, u32[]{:S(2)}, u32[]{:S(2)}) collective-permute-start(bf16[2,2,32,1024]{3,2,0,1:T(8,128)(2,1)S(1)} %fusion.10), channel_id=1, source_target_pairs={{0,4},{1,5},{2,6},{3,7},{4,0},{5,1},{6,2},{7,3},{8,12},{9,13},{10,... | collective-permute-start | bytes 786440 | tf_op jit(solution)/shard_map/ppermute | solution.py:114
  71.6 15.4 %collective-permute-start.7 = (bf16[2,32,1024]{2,1,0:T(8,128)(2,1)S(1)}, bf16[2,32,1024]{2,1,0:T(8,128)(2,1)S(1)}, u32[]{:S(2)}, u32[]{:S(2)}) collective-permute-start(bf16[2,32,1024]{2,1,0:T(8,128)(2,1)S(1)} %fusion.11), channel_id=1, source_target_pairs={{0,16},{1,17},{2,18},{3,19},{4,20},{5,21},{6,22},{7,23},{8,24},{9,... | collective-permute-start | bytes 393224 | tf_op jit(solution)/shard_map/ppermute | solution.py:114
  74.4 19.1 %collective-permute-start.11 = (bf16[2,2,32,1024]{3,2,0,1:T(8,128)(2,1)S(1)}, bf16[2,2,32,1024]{3,2,0,1:T(8,128)(2,1)S(1)}, u32[]{:S(2)}, u32[]{:S(2)}) collective-permute-start(bf16[2,2,32,1024]{3,2,0,1:T(8,128)(2,1)S(1)} %fusion.9), channel_id=1, source_target_pairs={{0,16},{1,17},{2,18},{3,19},{4,20},{5,21},{6,22},{7,23},{8,24},{9,... | collective-permute-start | bytes 786440 | tf_op jit(solution)/shard_map/ppermute | solution.py:114
  74.9 12.5 %collective-permute-start.17 = (bf16[2,32,1024]{2,1,0:T(8,128)(2,1)S(1)}, bf16[2,32,1024]{2,1,0:T(8,128)(2,1)S(1)}, u32[]{:S(2)}, u32[]{:S(2)}) collective-permute-start(bf16[2,32,1024]{2,1,0:T(8,128)(2,1)S(1)} %fusion.13), channel_id=1, source_target_pairs={{0,8},{1,9},{2,10},{3,11},{4,12},{5,13},{6,14},{7,15},{8,0},{9,1},... | collective-permute-start | bytes 393224 | tf_op jit(solution)/shard_map/ppermute | solution.py:114
  87.0 6.7 %collective-permute-start.8 = (bf16[32,1024]{1,0:T(8,128)(2,1)S(1)}, bf16[32,1024]{1,0:T(8,128)(2,1)S(1)}, u32[]{:S(2)}, u32[]{:S(2)}) collective-permute-start(bf16[32,1024]{1,0:T(8,128)(2,1)S(1)} %fusion.19), channel_id=1, source_target_pairs={{0,2},{1,3},{2,0},{3,1},{4,6},{5,7},{6,4},{7,5},{8,10},{9,11},{10,... | collective-permute-start | bytes 196616 | tf_op jit(solution)/shard_map/ppermute | solution.py:114
  87.5 11.8 %collective-permute-start.18 = (bf16[32,1024]{1,0:T(8,128)(2,1)S(1)}, bf16[32,1024]{1,0:T(8,128)(2,1)S(1)}, u32[]{:S(2)}, u32[]{:S(2)}) collective-permute-start(bf16[32,1024]{1,0:T(8,128)(2,1)S(1)} %fusion.21), channel_id=1, source_target_pairs={{0,16},{1,17},{2,18},{3,19},{4,20},{5,21},{6,22},{7,23},{8,24},{9,... | collective-permute-start | bytes 196616 | tf_op jit(solution)/shard_map/ppermute | solution.py:114
  93.7 5.0 %collective-permute-start.12 = (bf16[2,32,1024]{2,1,0:T(8,128)(2,1)S(1)}, bf16[2,32,1024]{2,1,0:T(8,128)(2,1)S(1)}, u32[]{:S(2)}, u32[]{:S(2)}) collective-permute-start(bf16[2,32,1024]{2,1,0:T(8,128)(2,1)S(1)} %fusion.12), channel_id=1, source_target_pairs={{0,2},{1,3},{2,0},{3,1},{4,6},{5,7},{6,4},{7,5},{8,10},{9,11},{10,... | collective-permute-start | bytes 393224 | tf_op jit(solution)/shard_map/ppermute | solution.py:114
  98.8 4.3 %collective-permute-start.13 = (bf16[32,1024]{1,0:T(8,128)(2,1)S(1)}, bf16[32,1024]{1,0:T(8,128)(2,1)S(1)}, u32[]{:S(2)}, u32[]{:S(2)}) collective-permute-start(bf16[32,1024]{1,0:T(8,128)(2,1)S(1)} %fusion.20), channel_id=1, source_target_pairs={{0,4},{1,5},{2,6},{3,7},{4,0},{5,1},{6,2},{7,3},{8,12},{9,13},{10,... | collective-permute-start | bytes 196616 | tf_op jit(solution)/shard_map/ppermute | solution.py:114

commit v2 on v1

--- a/solution.py
+++ b/solution.py
@@ -131,7 +131,7 @@
     far_back = passed_along(far_part, "seq", -2)
     bits = lax.axis_size("seq").bit_length() - 1
     rest = list(range(1, bits))
-    orders = ([0] + rest, [0] + rest[1:] + rest[:1], [0] + rest[2:] + rest[:2])
+    orders = ([0] + rest, [0] + rest[1::-1] + rest[2:], [0] + rest[2:] + rest[:2])
     out_rows = scattered_sum(dot(out_cotangent, attended, TN), "seq", orders[0])
     query_rows = scattered_sum(dot(tokens, query_grad, TN), "seq", orders[1])
     attn_out = dot(attended, out_weight, NN).astype(BF16)

time: 104 us -> 100 us (0.962)
  waiting for transfers between devices: 42.5 us -> 28.8 us
  starting transfers between devices: 30.8 us -> 40.7 us
    ppermute x15, waiting for transfers between devices: 37.7 us -> 24 us  [scattered_sum(): got = lax.ppermute(sent, axis, [(i, i ^ 1 << bit) for i in range(n)])]
    ppermute x15, starting transfers between devices: 21.2 us -> 31.2 us  [scattered_sum(): got = lax.ppermute(sent, axis, [(i, i ^ 1 << bit) for i in range(n)])]
  transfers between devices with their start and end apart: 19 -> 19, of which waited for: 8 -> 10; matrix products, arithmetic and copies ran while one was open for 15% -> 16% of each run, Pallas kernels for 0% -> 0%
where the time goes in v2:
time: 100 us
  starting transfers between devices  40.7 us (41%)
  waiting for transfers between devices  28.8 us (29%)
  matrix products  14.6 us (15%)
  Pallas kernels  8.95 us (9%)
  other arithmetic  3.5 us (4%)
  local copies, waits for them, and re-layouts  2.42 us (2%)
  between operations  1.08 us (1%)
    ppermute x15, starting transfers between devices, scattered_sum(): got = lax.ppermute(sent, axis, [(i, i ^ 1 << bit) for i in range(n)])  31.2 us
    ppermute x15, waiting for transfers between devices, scattered_sum(): got = lax.ppermute(sent, axis, [(i, i ^ 1 << bit) for i in range(n)])  24 us
    dot_general x11, matrix products, dot(): lax.dot_general(left, right, (dims, ((), ())), preferred_element_type=F32)  14.6 us
    ppermute x4, starting transfers between devices, passed_along(): return lax.ppermute(block, axis, route)  9.56 us
    pallas_call x1, Pallas kernels, attention(): pl.pallas_call(attention_kernel, out_shape=(shape(queries.shape, BF16), s...  8.95 us
    ppermute x4, waiting for transfers between devices, passed_along(): return lax.ppermute(block, axis, route)  4.79 us
    add x14, other arithmetic, scattered_sum(): held = kept.astype(F32) + got.astype(F32)  2.72 us
  transfers between devices with their start and end apart: 19, of which 10 were waited for; matrix products, arithmetic and copies ran while one was open for 16% of the time, Pallas kernels for 0%

profile of v2, /device:TPU:0, one launch (start us, length us, event | category | flops | bytes accessed | tf_op | source)
XLA Modules:
  0.0 100.0 jit_solution(6616609167848646462)
XLA Ops:
  0.7 1.8 %convolution_convert_fusion.3 = bf16[128,512]{1,0:T(8,128)(2,1)S(1)} fusion(bf16[128,1024]{1,0:T(8,128)(2,1)} %param.6, bf16[1024,512]{1,0:T(8,128)(2,1)} %param.9), kind=kOutput, calls=%fused_computation.12 | convolution fusion | flops 134283264 | bytes 1441792 | tf_op jit(solution)/shard_map/dot_general | solution.py:16
  2.4 1.7 %convolution_convert_fusion.4 = bf16[128,512]{1,0:T(8,128)(2,1)S(1)} fusion(bf16[128,1024]{1,0:T(8,128)(2,1)} %param.6, bf16[1024,512]{1,0:T(8,128)(2,1)} %param.8), kind=kOutput, calls=%fused_computation.13 | convolution fusion | flops 134283264 | bytes 1441792 | tf_op jit(solution)/shard_map/dot_general | solution.py:16
  4.1 2.4 %collective-permute-start = (bf16[128,1024]{1,0:T(8,128)(2,1)S(1)}, bf16[128,1024]{1,0:T(8,128)(2,1)S(1)}, u32[]{:S(2)}, u32[]{:S(2)}) collective-permute-start(bf16[128,1024]{1,0:T(8,128)(2,1)S(1)} %pad_maximum_fusion.own_ref), channel_id=1, source_target_pairs={{0,1},{1,2},{2,3},{3,4},{4,5},{5,6},{6,7},{7,8},{8,9},{9,10},{10,1... | collective-permute-start | bytes 786440 | tf_op jit(solution)/shard_map/ppermute | solution.py:27
  6.6 4.4 %collective-permute-start.1 = (bf16[128,1024]{1,0:T(8,128)(2,1)S(1)}, bf16[128,1024]{1,0:T(8,128)(2,1)S(1)}, u32[]{:S(2)}, u32[]{:S(2)}) collective-permute-start(bf16[128,1024]{1,0:T(8,128)(2,1)S(1)} %pad_maximum_fusion.own_ref), channel_id=1, source_target_pairs={{0,2},{1,3},{2,4},{3,5},{4,6},{5,7},{6,8},{7,9},{8,10},{9,11},{10,... | collective-permute-start | bytes 786440 | tf_op jit(solution)/shard_map/ppermute | solution.py:27
  11.0 2.7 %convolution_convert_fusion.2.q_ref = bf16[128,1024]{1,0:T(8,128)(2,1)} fusion(bf16[128,1024]{1,0:T(8,128)(2,1)S(1)} %copy-done.2, bf16[1024,1024]{1,0:T(8,128)(2,1)} %param.7), kind=kOutput, calls=%fused_computation.11 | convolution fusion | flops 268566528 | bytes 2621440 | tf_op jit(solution)/shard_map/dot_general | solution.py:16
  13.8 1.5 %convolution_convert_fusion.1.d_ref = bf16[128,1024]{1,0:T(8,128)(2,1)} fusion(bf16[128,1024]{1,0:T(8,128)(2,1)S(1)} %copy-done.6, bf16[1024,1024]{1,0:T(8,128)(2,1)S(1)} %copy-done), kind=kOutput, calls=%fused_computation.10 | convolution fusion | flops 268566528 | bytes 2621440 | tf_op jit(solution)/shard_map/dot_general | solution.py:16
  15.3 2.3 %collective-permute-done.1.far_ref = bf16[128,1024]{1,0:T(8,128)(2,1)S(1)} collective-permute-done((bf16[128,1024]{1,0:T(8,128)(2,1)S(1)}, bf16[128,1024]{1,0:T(8,128)(2,1)S(1)}, u32[]{:S(2)}, u32[]{:S(2)}) %collective-permute-start.1) | collective-permute-done | bytes 262176 | tf_op jit(solution)/shard_map/ppermute | solution.py:27
  17.6 0.7 copy-done.11
  18.4 8.9 %attention.1 = (bf16[128,1024]{1,0:T(8,128)(2,1)}, bf16[128,1024]{1,0:T(8,128)(2,1)}, f32[128,1024]{1,0:T(8,128)}, bf16[128,1024]{1,0:T(8,128)(2,1)}, bf16[128,1024]{1,0:T(8,128)(2,1)}) custom-call(bf16[128,1024]{1,0:T(8,128)(2,1)} %convolution_convert_fusion.2.q_ref, bf16[128,1024]{1,0:T(8,128)(2,1)} %copy-done.9, bf16[128,1024]{1,0:T(8,128)(2,1)} %copy-done.10, ...), custom_call_target="tpu_custom_call" | custom-call | flops 1000000000 | bytes 4000000 | tf_op jit(solution)/shard_map/attention/pallas_call | solution.py:85
  27.3 1.3 %collective-permute-start.3 = (bf16[128,1024]{1,0:T(8,128)(2,1)}, bf16[128,1024]{1,0:T(8,128)(2,1)S(1)}, u32[]{:S(2)}, u32[]{:S(2)}) collective-permute-start(bf16[128,1024]{1,0:T(8,128)(2,1)} %get-tuple-element.15), channel_id=1, source_target_pairs={{2,0},{3,1},{4,2},{5,3},{6,4},{7,5},{8,6},{9,7},{10,8},{11,9},{12,... | collective-permute-start | bytes 786440 | tf_op jit(solution)/shard_map/ppermute | solution.py:27
  28.6 1.5 %collective-permute-start.2 = (bf16[128,1024]{1,0:T(8,128)(2,1)}, bf16[128,1024]{1,0:T(8,128)(2,1)S(1)}, u32[]{:S(2)}, u32[]{:S(2)}) collective-permute-start(bf16[128,1024]{1,0:T(8,128)(2,1)} %get-tuple-element.14), channel_id=1, source_target_pairs={{1,0},{2,1},{3,2},{4,3},{5,4},{6,5},{7,6},{8,7},{9,8},{10,9},{11,1... | collective-permute-start | bytes 786440 | tf_op jit(solution)/shard_map/ppermute | solution.py:27
  30.1 1.7 %fusion.23 = f32[1024,1024]{0,1:T(8,128)S(1)} fusion(bf16[128,1024]{1,0:T(8,128)(2,1)} %get-tuple-element.12, bf16[128,1024]{1,0:T(8,128)(2,1)S(1)} %copy-done.2), kind=kOutput, calls=%fused_computation.67 | convolution fusion | flops 268435456 | bytes 4718592 | tf_op jit(solution)/shard_map/dot_general | solution.py:16
  32.0 1.2 %collective-permute-start.4 = (bf16[2,2,2,2,32,1024]{5,4,0,1,3,2:T(8,128)(2,1)S(1)}, bf16[2,2,2,2,32,1024]{5,4,0,1,3,2:T(8,128)(2,1)S(1)}, u32[]{:S(2)}, u32[]{:S(2)}) collective-permute-start(bf16[2,2,2,2,32,1024]{5,4,0,1,3,2:T(8,128)(2,1)S(1)} %fusion.2), channel_id=1, source_target_pairs={{0,1},{1,0},{2,3},{3,2},{4,5},{5,4},{6,7},{7,6},{8,9},{9,8},{10,11... | collective-permute-start | bytes 3145736 | tf_op jit(solution)/shard_map/ppermute | solution.py:114
  33.2 0.8 fusion.25
  34.1 0.8 collective-permute-start.14
  34.9 1.2 %convolution_convert_fusion = bf16[128,1024]{1,0:T(8,128)(2,1)} fusion(bf16[128,1024]{1,0:T(8,128)(2,1)S(1)} %copy-done.7, bf16[1024,1024]{1,0:T(8,128)(2,1)S(1)} %copy-done), kind=kOutput, calls=%fused_computation.9 | convolution fusion | flops 268566528 | bytes 2621440 | tf_op jit(solution)/shard_map/dot_general | solution.py:16
  36.0 2.5 %collective-permute-done.3 = bf16[128,1024]{1,0:T(8,128)(2,1)S(1)} collective-permute-done((bf16[128,1024]{1,0:T(8,128)(2,1)}, bf16[128,1024]{1,0:T(8,128)(2,1)S(1)}, u32[]{:S(2)}, u32[]{:S(2)}) %collective-permute-start.3) | collective-permute-done | bytes 262176 | tf_op jit(solution)/shard_map/ppermute | solution.py:27
  38.6 0.5 fusion.14
  39.1 0.8 fusion.24
  40.1 2.7 %collective-permute-start.9 = (bf16[2,2,2,2,32,1024]{5,4,2,3,0,1:T(8,128)(2,1)S(1)}, bf16[2,2,2,2,32,1024]{5,4,2,3,0,1:T(8,128)(2,1)S(1)}, u32[]{:S(2)}, u32[]{:S(2)}) collective-permute-start(bf16[2,2,2,2,32,1024]{5,4,2,3,0,1:T(8,128)(2,1)S(1)} %fusion.3), channel_id=1, source_target_pairs={{0,1},{1,0},{2,3},{3,2},{4,5},{5,4},{6,7},{7,6},{8,9},{9,8},{10,11... | collective-permute-start | bytes 3145736 | tf_op jit(solution)/shard_map/ppermute | solution.py:114
  42.8 0.5 fusion.16
  43.2 1.6 %fusion.1 = bf16[128,1024]{1,0:T(8,128)(2,1)} fusion(f32[128,1024]{1,0:T(8,128)S(1)} %fusion.14, f32[128,1024]{1,0:T(8,128)S(1)} %fusion.16, bf16[128,1024]{1,0:T(8,128)(2,1)S(1)} %copy-done.5, bf16[1024,1024]{1,0:T(8,128)(2,1)S(1)} %copy-done.1), kind=kOutput, calls=%fused_computation.8 | convolution fusion | flops 268828672 | bytes 3670016 | tf_op jit(solution)/shard_map/dot_general | solution.py:16
  44.8 0.5 bitcast_add_fusion.2
  45.4 2.7 %collective-permute-start.5 = (bf16[2,2,2,32,1024]{4,3,0,1,2:T(8,128)(2,1)S(1)}, bf16[2,2,2,32,1024]{4,3,0,1,2:T(8,128)(2,1)S(1)}, u32[]{:S(2)}, u32[]{:S(2)}) collective-permute-start(bf16[2,2,2,32,1024]{4,3,0,1,2:T(8,128)(2,1)S(1)} %fusion.5), channel_id=1, source_target_pairs={{0,4},{1,5},{2,6},{3,7},{4,0},{5,1},{6,2},{7,3},{8,12},{9,13},{10,... | collective-permute-start | bytes 1572872 | tf_op jit(solution)/shard_map/ppermute | solution.py:114
  48.1 0.5 bitcast_add_fusion
  48.6 2.4 %collective-permute-start.15 = (bf16[2,2,2,32,1024]{4,3,0,1,2:T(8,128)(2,1)S(1)}, bf16[2,2,2,32,1024]{4,3,0,1,2:T(8,128)(2,1)S(1)}, u32[]{:S(2)}, u32[]{:S(2)}) collective-permute-start(bf16[2,2,2,32,1024]{4,3,0,1,2:T(8,128)(2,1)S(1)} %fusion.7), channel_id=1, source_target_pairs={{0,2},{1,3},{2,0},{3,1},{4,6},{5,7},{6,4},{7,5},{8,10},{9,11},{10,... | collective-permute-start | bytes 1572872 | tf_op jit(solution)/shard_map/ppermute | solution.py:114
  51.1 0.5 bitcast_add_fusion.1
  51.6 1.7 %collective-permute-start.10 = (bf16[2,2,2,32,1024]{4,3,1,2,0:T(8,128)(2,1)S(1)}, bf16[2,2,2,32,1024]{4,3,1,2,0:T(8,128)(2,1)S(1)}, u32[]{:S(2)}, u32[]{:S(2)}) collective-permute-start(bf16[2,2,2,32,1024]{4,3,1,2,0:T(8,128)(2,1)S(1)} %fusion.6), channel_id=1, source_target_pairs={{0,8},{1,9},{2,10},{3,11},{4,12},{5,13},{6,14},{7,15},{8,0},{9,1},... | collective-permute-start | bytes 1572872 | tf_op jit(solution)/shard_map/ppermute | solution.py:114
  53.3 7.4 %collective-permute-done.5 = bf16[2,2,2,32,1024]{4,3,0,1,2:T(8,128)(2,1)S(1)} collective-permute-done((bf16[2,2,2,32,1024]{4,3,0,1,2:T(8,128)(2,1)S(1)}, bf16[2,2,2,32,1024]{4,3,0,1,2:T(8,128)(2,1)S(1)}, u32[]{:S(2)}, u32[]{:S(2)}) %collective-permute-start.5) | collective-permute-done | bytes 524320 | tf_op jit(solution)/shard_map/ppermute | solution.py:114
  60.8 2.4 %collective-permute-start.6 = (bf16[2,2,32,1024]{3,2,0,1:T(8,128)(2,1)S(1)}, bf16[2,2,32,1024]{3,2,0,1:T(8,128)(2,1)S(1)}, u32[]{:S(2)}, u32[]{:S(2)}) collective-permute-start(bf16[2,2,32,1024]{3,2,0,1:T(8,128)(2,1)S(1)} %fusion.8), channel_id=1, source_target_pairs={{0,2},{1,3},{2,0},{3,1},{4,6},{5,7},{6,4},{7,5},{8,10},{9,11},{10,... | collective-permute-start | bytes 786440 | tf_op jit(solution)/shard_map/ppermute | solution.py:114
  63.3 0.5 collective-permute-done.15
  64.0 1.7 %collective-permute-start.16 = (bf16[2,2,32,1024]{3,2,0,1:T(8,128)(2,1)S(1)}, bf16[2,2,32,1024]{3,2,0,1:T(8,128)(2,1)S(1)}, u32[]{:S(2)}, u32[]{:S(2)}) collective-permute-start(bf16[2,2,32,1024]{3,2,0,1:T(8,128)(2,1)S(1)} %fusion.10), channel_id=1, source_target_pairs={{0,4},{1,5},{2,6},{3,7},{4,0},{5,1},{6,2},{7,3},{8,12},{9,13},{10,... | collective-permute-start | bytes 786440 | tf_op jit(solution)/shard_map/ppermute | solution.py:114
  65.7 4.4 %collective-permute-done.6 = bf16[2,2,32,1024]{3,2,0,1:T(8,128)(2,1)S(1)} collective-permute-done((bf16[2,2,32,1024]{3,2,0,1:T(8,128)(2,1)S(1)}, bf16[2,2,32,1024]{3,2,0,1:T(8,128)(2,1)S(1)}, u32[]{:S(2)}, u32[]{:S(2)}) %collective-permute-start.6) | collective-permute-done | bytes 262176 | tf_op jit(solution)/shard_map/ppermute | solution.py:114
  70.2 2.3 %collective-permute-start.7 = (bf16[2,32,1024]{2,1,0:T(8,128)(2,1)S(1)}, bf16[2,32,1024]{2,1,0:T(8,128)(2,1)S(1)}, u32[]{:S(2)}, u32[]{:S(2)}) collective-permute-start(bf16[2,32,1024]{2,1,0:T(8,128)(2,1)S(1)} %fusion.11), channel_id=1, source_target_pairs={{0,8},{1,9},{2,10},{3,11},{4,12},{5,13},{6,14},{7,15},{8,0},{9,1},... | collective-permute-start | bytes 393224 | tf_op jit(solution)/shard_map/ppermute | solution.py:114
  72.7 2.7 %collective-permute-start.11 = (bf16[2,2,32,1024]{3,2,0,1:T(8,128)(2,1)S(1)}, bf16[2,2,32,1024]{3,2,0,1:T(8,128)(2,1)S(1)}, u32[]{:S(2)}, u32[]{:S(2)}) collective-permute-start(bf16[2,2,32,1024]{3,2,0,1:T(8,128)(2,1)S(1)} %fusion.9), channel_id=1, source_target_pairs={{0,16},{1,17},{2,18},{3,19},{4,20},{5,21},{6,22},{7,23},{8,24},{9,... | collective-permute-start | bytes 786440 | tf_op jit(solution)/shard_map/ppermute | solution.py:114
  75.4 0.5 collective-permute-start.17
  75.9 0.5 collective-permute-done.7
  76.5 3.9 %collective-permute-start.8 = (bf16[32,1024]{1,0:T(8,128)(2,1)S(1)}, bf16[32,1024]{1,0:T(8,128)(2,1)S(1)}, u32[]{:S(2)}, u32[]{:S(2)}) collective-permute-start(bf16[32,1024]{1,0:T(8,128)(2,1)S(1)} %fusion.19), channel_id=1, source_target_pairs={{0,16},{1,17},{2,18},{3,19},{4,20},{5,21},{6,22},{7,23},{8,24},{9,... | collective-permute-start | bytes 196616 | tf_op jit(solution)/shard_map/ppermute | solution.py:114
  80.4 3.7 %collective-permute-done.17 = bf16[2,32,1024]{2,1,0:T(8,128)(2,1)S(1)} collective-permute-done((bf16[2,32,1024]{2,1,0:T(8,128)(2,1)S(1)}, bf16[2,32,1024]{2,1,0:T(8,128)(2,1)S(1)}, u32[]{:S(2)}, u32[]{:S(2)}) %collective-permute-start.17) | collective-permute-done | bytes 131104 | tf_op jit(solution)/shard_map/ppermute | solution.py:114
  84.2 3.1 %collective-permute-start.18 = (bf16[32,1024]{1,0:T(8,128)(2,1)S(1)}, bf16[32,1024]{1,0:T(8,128)(2,1)S(1)}, u32[]{:S(2)}, u32[]{:S(2)}) collective-permute-start(bf16[32,1024]{1,0:T(8,128)(2,1)S(1)} %fusion.21), channel_id=1, source_target_pairs={{0,16},{1,17},{2,18},{3,19},{4,20},{5,21},{6,22},{7,23},{8,24},{9,... | collective-permute-start | bytes 196616 | tf_op jit(solution)/shard_map/ppermute | solution.py:114
  87.3 2.5 %collective-permute-done.11 = bf16[2,2,32,1024]{3,2,0,1:T(8,128)(2,1)S(1)} collective-permute-done((bf16[2,2,32,1024]{3,2,0,1:T(8,128)(2,1)S(1)}, bf16[2,2,32,1024]{3,2,0,1:T(8,128)(2,1)S(1)}, u32[]{:S(2)}, u32[]{:S(2)}) %collective-permute-start.11) | collective-permute-done | bytes 262176 | tf_op jit(solution)/shard_map/ppermute | solution.py:114
  89.9 1.5 %collective-permute-start.12 = (bf16[2,32,1024]{2,1,0:T(8,128)(2,1)S(1)}, bf16[2,32,1024]{2,1,0:T(8,128)(2,1)S(1)}, u32[]{:S(2)}, u32[]{:S(2)}) collective-permute-start(bf16[2,32,1024]{2,1,0:T(8,128)(2,1)S(1)} %fusion.12), channel_id=1, source_target_pairs={{0,2},{1,3},{2,0},{3,1},{4,6},{5,7},{6,4},{7,5},{8,10},{9,11},{10,... | collective-permute-start | bytes 393224 | tf_op jit(solution)/shard_map/ppermute | solution.py:114
  91.4 0.7 bitcast_add_fusion.14
  92.0 2.9 %collective-permute-done.12 = bf16[2,32,1024]{2,1,0:T(8,128)(2,1)S(1)} collective-permute-done((bf16[2,32,1024]{2,1,0:T(8,128)(2,1)S(1)}, bf16[2,32,1024]{2,1,0:T(8,128)(2,1)S(1)}, u32[]{:S(2)}, u32[]{:S(2)}) %collective-permute-start.12) | collective-permute-done | bytes 131104 | tf_op jit(solution)/shard_map/ppermute | solution.py:114
  95.0 1.6 %collective-permute-start.13 = (bf16[32,1024]{1,0:T(8,128)(2,1)S(1)}, bf16[32,1024]{1,0:T(8,128)(2,1)S(1)}, u32[]{:S(2)}, u32[]{:S(2)}) collective-permute-start(bf16[32,1024]{1,0:T(8,128)(2,1)S(1)} %fusion.20), channel_id=1, source_target_pairs={{0,4},{1,5},{2,6},{3,7},{4,0},{5,1},{6,2},{7,3},{8,12},{9,13},{10,... | collective-permute-start | bytes 196616 | tf_op jit(solution)/shard_map/ppermute | solution.py:114
  96.6 0.7 fusion.18
  97.3 2.0 %collective-permute-done.13 = bf16[32,1024]{1,0:T(8,128)(2,1)S(1)} collective-permute-done((bf16[32,1024]{1,0:T(8,128)(2,1)S(1)}, bf16[32,1024]{1,0:T(8,128)(2,1)S(1)}, u32[]{:S(2)}, u32[]{:S(2)}) %collective-permute-start.13) | collective-permute-done | bytes 65568 | tf_op jit(solution)/shard_map/ppermute | solution.py:114
  99.3 0.7 fusion.22
  (59 shorter events, 1.9 us)
Async XLA Ops:
  0.6 13.1 %copy-start = (bf16[1024,1024]{1,0:T(8,128)(2,1)S(1)}, bf16[1024,1024]{1,0:T(8,128)(2,1)}, u32[]{:S(2)}) copy-start(bf16[1024,1024]{1,0:T(8,128)(2,1)} %param.10) | copy-start | bytes 6291460
  0.6 10.3 %copy-start.2 = (bf16[128,1024]{1,0:T(8,128)(2,1)S(1)}, bf16[128,1024]{1,0:T(8,128)(2,1)}, u32[]{:S(2)}) copy-start(bf16[128,1024]{1,0:T(8,128)(2,1)} %param.6) | copy-start | bytes 786436
  2.4 11.3 %copy-start.6 = (bf16[128,1024]{1,0:T(8,128)(2,1)S(1)}, bf16[128,1024]{1,0:T(8,128)(2,1)}, u32[]{:S(2)}) copy-start(bf16[128,1024]{1,0:T(8,128)(2,1)} %param.11) | copy-start | bytes 786436
  4.1 11.2 %copy-start.9 = (bf16[128,1024]{1,0:T(8,128)(2,1)}, bf16[128,1024]{1,0:T(8,128)(2,1)S(1)}, u32[]{:S(2)}) copy-start(bf16[128,1024]{1,0:T(8,128)(2,1)S(1)} %pad_maximum_fusion.own_ref) | copy-start | bytes 786436
  4.1 11.1 %collective-permute-start = (bf16[128,1024]{1,0:T(8,128)(2,1)S(1)}, bf16[128,1024]{1,0:T(8,128)(2,1)S(1)}, u32[]{:S(2)}, u32[]{:S(2)}) collective-permute-start(bf16[128,1024]{1,0:T(8,128)(2,1)S(1)} %pad_maximum_fusion.own_ref), channel_id=1, source_target_pairs={{0,1},{1,2},{2,3},{3,4},{4,5},{5,6},{6,7},{7,8},{8,9},{9,10},{10,1... | collective-permute-start | bytes 786440 | tf_op jit(solution)/shard_map/ppermute | solution.py:27
  6.6 11.1 %collective-permute-start.1 = (bf16[128,1024]{1,0:T(8,128)(2,1)S(1)}, bf16[128,1024]{1,0:T(8,128)(2,1)S(1)}, u32[]{:S(2)}, u32[]{:S(2)}) collective-permute-start(bf16[128,1024]{1,0:T(8,128)(2,1)S(1)} %pad_maximum_fusion.own_ref), channel_id=1, source_target_pairs={{0,2},{1,3},{2,4},{3,5},{4,6},{5,7},{6,8},{7,9},{8,10},{9,11},{10,... | collective-permute-start | bytes 786440 | tf_op jit(solution)/shard_map/ppermute | solution.py:27
  15.3 2.3 %copy-start.10 = (bf16[128,1024]{1,0:T(8,128)(2,1)}, bf16[128,1024]{1,0:T(8,128)(2,1)S(1)}, u32[]{:S(2)}) copy-start(bf16[128,1024]{1,0:T(8,128)(2,1)S(1)} %collective-permute-done.near_ref) | copy-start | bytes 786436
  17.6 0.7 copy-start.11
  27.3 11.2 %collective-permute-start.3 = (bf16[128,1024]{1,0:T(8,128)(2,1)}, bf16[128,1024]{1,0:T(8,128)(2,1)S(1)}, u32[]{:S(2)}, u32[]{:S(2)}) collective-permute-start(bf16[128,1024]{1,0:T(8,128)(2,1)} %get-tuple-element.15), channel_id=1, source_target_pairs={{2,0},{3,1},{4,2},{5,3},{6,4},{7,5},{8,6},{9,7},{10,8},{11,9},{12,... | collective-permute-start | bytes 786440 | tf_op jit(solution)/shard_map/ppermute | solution.py:27
  28.6 9.9 %collective-permute-start.2 = (bf16[128,1024]{1,0:T(8,128)(2,1)}, bf16[128,1024]{1,0:T(8,128)(2,1)S(1)}, u32[]{:S(2)}, u32[]{:S(2)}) collective-permute-start(bf16[128,1024]{1,0:T(8,128)(2,1)} %get-tuple-element.14), channel_id=1, source_target_pairs={{1,0},{2,1},{3,2},{4,3},{5,4},{6,5},{7,6},{8,7},{9,8},{10,9},{11,1... | collective-permute-start | bytes 786440 | tf_op jit(solution)/shard_map/ppermute | solution.py:27
  31.8 1.4 %copy-start.7 = (bf16[128,1024]{1,0:T(8,128)(2,1)S(1)}, bf16[128,1024]{1,0:T(8,128)(2,1)}, u32[]{:S(2)}) copy-start(bf16[128,1024]{1,0:T(8,128)(2,1)} %get-tuple-element.11) | copy-start | bytes 786436
  32.0 12.9 %collective-permute-start.4 = (bf16[2,2,2,2,32,1024]{5,4,0,1,3,2:T(8,128)(2,1)S(1)}, bf16[2,2,2,2,32,1024]{5,4,0,1,3,2:T(8,128)(2,1)S(1)}, u32[]{:S(2)}, u32[]{:S(2)}) collective-permute-start(bf16[2,2,2,2,32,1024]{5,4,0,1,3,2:T(8,128)(2,1)S(1)} %fusion.2), channel_id=1, source_target_pairs={{0,1},{1,0},{2,3},{3,2},{4,5},{5,4},{6,7},{7,6},{8,9},{9,8},{10,11... | collective-permute-start | bytes 3145736 | tf_op jit(solution)/shard_map/ppermute | solution.py:114
  33.9 4.6 %copy-start.8 = (f32[128,1024]{1,0:T(8,128)S(1)}, f32[128,1024]{1,0:T(8,128)}, u32[]{:S(2)}) copy-start(f32[128,1024]{1,0:T(8,128)} %get-tuple-element.13) | copy-start | bytes 1572868
  34.1 4.5 %copy-start.3 = (bf16[1024,512]{1,0:T(8,128)(2,1)S(1)}, bf16[1024,512]{1,0:T(8,128)(2,1)}, u32[]{:S(2)}) copy-start(bf16[1024,512]{1,0:T(8,128)(2,1)} %param.9) | copy-start | bytes 3145732
  34.1 14.0 %collective-permute-start.14 = (bf16[2,2,2,2,32,1024]{5,4,0,1,2,3:T(8,128)(2,1)S(1)}, bf16[2,2,2,2,32,1024]{5,4,0,1,2,3:T(8,128)(2,1)S(1)}, u32[]{:S(2)}, u32[]{:S(2)}) collective-permute-start(bf16[2,2,2,2,32,1024]{5,4,0,1,2,3:T(8,128)(2,1)S(1)} %fusion.4), channel_id=1, source_target_pairs={{0,1},{1,0},{2,3},{3,2},{4,5},{5,4},{6,7},{7,6},{8,9},{9,8},{10,11... | collective-permute-start | bytes 3145736 | tf_op jit(solution)/shard_map/ppermute | solution.py:114
  39.1 3.7 %copy-start.4 = (bf16[1024,512]{1,0:T(8,128)(2,1)S(1)}, bf16[1024,512]{1,0:T(8,128)(2,1)}, u32[]{:S(2)}) copy-start(bf16[1024,512]{1,0:T(8,128)(2,1)} %param.8) | copy-start | bytes 3145732
  39.9 3.4 %copy-start.1 = (bf16[1024,1024]{1,0:T(8,128)(2,1)S(1)}, bf16[1024,1024]{1,0:T(8,128)(2,1)}, u32[]{:S(2)}) copy-start(bf16[1024,1024]{1,0:T(8,128)(2,1)} %param.7) | copy-start | bytes 6291460
  39.9 3.4 %copy-start.5 = (bf16[128,1024]{1,0:T(8,128)(2,1)S(1)}, bf16[128,1024]{1,0:T(8,128)(2,1)}, u32[]{:S(2)}) copy-start(bf16[128,1024]{1,0:T(8,128)(2,1)} %get-tuple-element.12) | copy-start | bytes 786436
  40.1 11.0 %collective-permute-start.9 = (bf16[2,2,2,2,32,1024]{5,4,2,3,0,1:T(8,128)(2,1)S(1)}, bf16[2,2,2,2,32,1024]{5,4,2,3,0,1:T(8,128)(2,1)S(1)}, u32[]{:S(2)}, u32[]{:S(2)}) collective-permute-start(bf16[2,2,2,2,32,1024]{5,4,2,3,0,1:T(8,128)(2,1)S(1)} %fusion.3), channel_id=1, source_target_pairs={{0,1},{1,0},{2,3},{3,2},{4,5},{5,4},{6,7},{7,6},{8,9},{9,8},{10,11... | collective-permute-start | bytes 3145736 | tf_op jit(solution)/shard_map/ppermute | solution.py:114
  45.4 15.3 %collective-permute-start.5 = (bf16[2,2,2,32,1024]{4,3,0,1,2:T(8,128)(2,1)S(1)}, bf16[2,2,2,32,1024]{4,3,0,1,2:T(8,128)(2,1)S(1)}, u32[]{:S(2)}, u32[]{:S(2)}) collective-permute-start(bf16[2,2,2,32,1024]{4,3,0,1,2:T(8,128)(2,1)S(1)} %fusion.5), channel_id=1, source_target_pairs={{0,4},{1,5},{2,6},{3,7},{4,0},{5,1},{6,2},{7,3},{8,12},{9,13},{10,... | collective-permute-start | bytes 1572872 | tf_op jit(solution)/shard_map/ppermute | solution.py:114
  48.6 15.2 %collective-permute-start.15 = (bf16[2,2,2,32,1024]{4,3,0,1,2:T(8,128)(2,1)S(1)}, bf16[2,2,2,32,1024]{4,3,0,1,2:T(8,128)(2,1)S(1)}, u32[]{:S(2)}, u32[]{:S(2)}) collective-permute-start(bf16[2,2,2,32,1024]{4,3,0,1,2:T(8,128)(2,1)S(1)} %fusion.7), channel_id=1, source_target_pairs={{0,2},{1,3},{2,0},{3,1},{4,6},{5,7},{6,4},{7,5},{8,10},{9,11},{10,... | collective-permute-start | bytes 1572872 | tf_op jit(solution)/shard_map/ppermute | solution.py:114
  51.6 20.8 %collective-permute-start.10 = (bf16[2,2,2,32,1024]{4,3,1,2,0:T(8,128)(2,1)S(1)}, bf16[2,2,2,32,1024]{4,3,1,2,0:T(8,128)(2,1)S(1)}, u32[]{:S(2)}, u32[]{:S(2)}) collective-permute-start(bf16[2,2,2,32,1024]{4,3,1,2,0:T(8,128)(2,1)S(1)} %fusion.6), channel_id=1, source_target_pairs={{0,8},{1,9},{2,10},{3,11},{4,12},{5,13},{6,14},{7,15},{8,0},{9,1},... | collective-permute-start | bytes 1572872 | tf_op jit(solution)/shard_map/ppermute | solution.py:114
  60.8 9.2 %collective-permute-start.6 = (bf16[2,2,32,1024]{3,2,0,1:T(8,128)(2,1)S(1)}, bf16[2,2,32,1024]{3,2,0,1:T(8,128)(2,1)S(1)}, u32[]{:S(2)}, u32[]{:S(2)}) collective-permute-start(bf16[2,2,32,1024]{3,2,0,1:T(8,128)(2,1)S(1)} %fusion.8), channel_id=1, source_target_pairs={{0,2},{1,3},{2,0},{3,1},{4,6},{5,7},{6,4},{7,5},{8,10},{9,11},{10,... | collective-permute-start | bytes 786440 | tf_op jit(solution)/shard_map/ppermute | solution.py:114
  64.0 11.3 %collective-permute-start.16 = (bf16[2,2,32,1024]{3,2,0,1:T(8,128)(2,1)S(1)}, bf16[2,2,32,1024]{3,2,0,1:T(8,128)(2,1)S(1)}, u32[]{:S(2)}, u32[]{:S(2)}) collective-permute-start(bf16[2,2,32,1024]{3,2,0,1:T(8,128)(2,1)S(1)} %fusion.10), channel_id=1, source_target_pairs={{0,4},{1,5},{2,6},{3,7},{4,0},{5,1},{6,2},{7,3},{8,12},{9,13},{10,... | collective-permute-start | bytes 786440 | tf_op jit(solution)/shard_map/ppermute | solution.py:114
  70.2 6.3 %collective-permute-start.7 = (bf16[2,32,1024]{2,1,0:T(8,128)(2,1)S(1)}, bf16[2,32,1024]{2,1,0:T(8,128)(2,1)S(1)}, u32[]{:S(2)}, u32[]{:S(2)}) collective-permute-start(bf16[2,32,1024]{2,1,0:T(8,128)(2,1)S(1)} %fusion.11), channel_id=1, source_target_pairs={{0,8},{1,9},{2,10},{3,11},{4,12},{5,13},{6,14},{7,15},{8,0},{9,1},... | collective-permute-start | bytes 393224 | tf_op jit(solution)/shard_map/ppermute | solution.py:114
  72.7 17.1 %collective-permute-start.11 = (bf16[2,2,32,1024]{3,2,0,1:T(8,128)(2,1)S(1)}, bf16[2,2,32,1024]{3,2,0,1:T(8,128)(2,1)S(1)}, u32[]{:S(2)}, u32[]{:S(2)}) collective-permute-start(bf16[2,2,32,1024]{3,2,0,1:T(8,128)(2,1)S(1)} %fusion.9), channel_id=1, source_target_pairs={{0,16},{1,17},{2,18},{3,19},{4,20},{5,21},{6,22},{7,23},{8,24},{9,... | collective-permute-start | bytes 786440 | tf_op jit(solution)/shard_map/ppermute | solution.py:114
  75.4 8.7 %collective-permute-start.17 = (bf16[2,32,1024]{2,1,0:T(8,128)(2,1)S(1)}, bf16[2,32,1024]{2,1,0:T(8,128)(2,1)S(1)}, u32[]{:S(2)}, u32[]{:S(2)}) collective-permute-start(bf16[2,32,1024]{2,1,0:T(8,128)(2,1)S(1)} %fusion.13), channel_id=1, source_target_pairs={{0,8},{1,9},{2,10},{3,11},{4,12},{5,13},{6,14},{7,15},{8,0},{9,1},... | collective-permute-start | bytes 393224 | tf_op jit(solution)/shard_map/ppermute | solution.py:114
  76.5 14.8 %collective-permute-start.8 = (bf16[32,1024]{1,0:T(8,128)(2,1)S(1)}, bf16[32,1024]{1,0:T(8,128)(2,1)S(1)}, u32[]{:S(2)}, u32[]{:S(2)}) collective-permute-start(bf16[32,1024]{1,0:T(8,128)(2,1)S(1)} %fusion.19), channel_id=1, source_target_pairs={{0,16},{1,17},{2,18},{3,19},{4,20},{5,21},{6,22},{7,23},{8,24},{9,... | collective-permute-start | bytes 196616 | tf_op jit(solution)/shard_map/ppermute | solution.py:114
  84.2 12.4 %collective-permute-start.18 = (bf16[32,1024]{1,0:T(8,128)(2,1)S(1)}, bf16[32,1024]{1,0:T(8,128)(2,1)S(1)}, u32[]{:S(2)}, u32[]{:S(2)}) collective-permute-start(bf16[32,1024]{1,0:T(8,128)(2,1)S(1)} %fusion.21), channel_id=1, source_target_pairs={{0,16},{1,17},{2,18},{3,19},{4,20},{5,21},{6,22},{7,23},{8,24},{9,... | collective-permute-start | bytes 196616 | tf_op jit(solution)/shard_map/ppermute | solution.py:114
  89.9 5.0 %collective-permute-start.12 = (bf16[2,32,1024]{2,1,0:T(8,128)(2,1)S(1)}, bf16[2,32,1024]{2,1,0:T(8,128)(2,1)S(1)}, u32[]{:S(2)}, u32[]{:S(2)}) collective-permute-start(bf16[2,32,1024]{2,1,0:T(8,128)(2,1)S(1)} %fusion.12), channel_id=1, source_target_pairs={{0,2},{1,3},{2,0},{3,1},{4,6},{5,7},{6,4},{7,5},{8,10},{9,11},{10,... | collective-permute-start | bytes 393224 | tf_op jit(solution)/shard_map/ppermute | solution.py:114
  95.0 4.3 %collective-permute-start.13 = (bf16[32,1024]{1,0:T(8,128)(2,1)S(1)}, bf16[32,1024]{1,0:T(8,128)(2,1)S(1)}, u32[]{:S(2)}, u32[]{:S(2)}) collective-permute-start(bf16[32,1024]{1,0:T(8,128)(2,1)S(1)} %fusion.20), channel_id=1, source_target_pairs={{0,4},{1,5},{2,6},{3,7},{4,0},{5,1},{6,2},{7,3},{8,12},{9,13},{10,... | collective-permute-start | bytes 196616 | tf_op jit(solution)/shard_map/ppermute | solution.py:114
